TPU v7x, 512 devices: a whole 4x4x16 slice. The times are simulated.
512 devices in a mesh: tm: 32 (over z, core), net: 16 (over y, x).
Axes of the slice: x: 4, y: 4, z: 16, core: 2. Of those that a mesh axis runs over, the one named last changes fastest.
Arguments:
- ptdf: bfloat16 [16384, 4096], P('net'), may hold values from -0.09375 to 0.09375
- demand: float32 [4096, 2048], P('net', 'tm'), may hold values from 0 to 2
- generation: float32 [4096, 2048], P('net', 'tm'), may hold values from 0 to 2
- cost: float32 [4096, 2048], P('net', 'tm'), may hold values from 0.2 to 4
- gen_cap: float32 [4096], P('net'), may hold values from 0.5 to 4
- storage: float32 [2048, 2048], P('net', 'tm'), may hold values from -3 to 3
- wear: float32 [2048], P('net'), may hold values from 0.1 to 2
- initial_charge: float32 [2048], P('net'), may hold values from 0 to 2
- leakage: float32 [2048], P('net'), may hold values from 0.00014648438 to 0.05
- line_dual: float32 [16384, 2048], P('net', 'tm'), may hold values from -3 to 3
- line_index: int32 [16384], P('net'), may hold values from 0 to 4095
- rating: float32 [4096], replicated, may hold values from 0.3 to 3
- storage_bus: int32 [2048], replicated, may hold values from 0 to 4095
- balance_dual: float32 [2048], P('tm'), may hold values from -4 to 4
- hour_block: int32 [2048], P('tm'), may hold values from 0 to 23
- block_price: float32 [24], replicated, may hold values from -4 to 4
Outputs:
- generation_next: float32 [4096, 2048], P('net', 'tm')
- storage_next: float32 [2048, 2048], P('net', 'tm')
- charge: float32 [2048, 2048], P('net', 'tm')
- line_dual_next: float32 [16384, 2048], P('net', 'tm')
- balance_price: float32 [2048], P('tm')
All inputs are finite; a program needn't handle non-finite values.
Results may differ from a plain program's by a relative error of at most 0.0028.
Values may be sent and summed in bfloat16 or wider, within the bound.
No kernel may reach another device: no remote copies, remote signals or barrier semaphores. Data moves between devices by JAX's collectives and lax.ppermute only.
A program may use at most 64 MiB of HBM per device.

v0:
```python
import jax
import jax.numpy as jnp
from jax import lax
from jax.sharding import Mesh
from jax.sharding import PartitionSpec as P

PASSES = 2
TM = ("tm_0", "tm_1")


STEP = 0.1
BAL = 0.5
STEP_UNIT = 0.2
ETA = 0.0625


def laid_out(parts, dim):
    lengths = list(parts.shape[1:])
    lengths[dim] *= parts.shape[0]
    return jnp.moveaxis(parts, 0, dim).reshape(lengths)


def sent_to_all(shard, axis):
    copies = jnp.broadcast_to(shard, (lax.axis_size(axis), *shard.shape))
    return lax.all_to_all(copies, axis, split_axis=0, concat_axis=0, tiled=True)


def gather_directly(shard, axis, dim):
    return laid_out(sent_to_all(shard, axis), dim)


def in_blocks(shard, dim, count):
    lengths = shard.shape
    parts = shard.reshape(*lengths[:dim], count, lengths[dim] // count, *lengths[dim + 1 :])
    return jnp.moveaxis(parts, dim, 0)


def summed_on_arrival(shard, axis, dim):
    parts = in_blocks(shard, dim, lax.axis_size(axis))
    arrived = lax.all_to_all(parts, axis, split_axis=0, concat_axis=0, tiled=True)
    return arrived.astype(jnp.float32).sum(axis=0)


def of_everyone(shard, axis):
    everything = sent_to_all(shard, axis)
    return jnp.sum(everything, axis=0)


def in_one(arrays, axis):
    flat, at, finished = (jnp.concatenate([a.reshape(-1) for a in arrays]), 0, [])
    subtotal = of_everyone(flat, axis)
    for a in arrays:
        finished.append(subtotal[at : at + a.size].reshape(a.shape))
        at += a.size
    return tuple(finished)


def neutral_like(shard, identity):
    return jax.tree.map(
        lambda a, e: jnp.broadcast_to(jnp.asarray(e, a.dtype), a.shape), shard, identity
    )


def gathered_once(shard, axis):
    leaves = jax.tree.leaves(shard)
    turns = sorted(range(len(leaves)), key=lambda k: -leaves[k].size)
    width = (1, *leaves[turns[0]].shape)[-1]
    lines = [
        jnp.pad(leaves[k].reshape(-1), (0, -leaves[k].size % width)).reshape(-1, width)
        for k in turns
    ]
    both, at, found = (lax.all_gather(jnp.concatenate(lines), axis), 0, {})
    for k, line in zip(turns, lines):
        piece = both[:, at : at + len(line)].reshape(len(both), -1)
        found[k] = piece[:, : leaves[k].size].reshape(-1, *leaves[k].shape)
        at += len(line)
    numbers = iter(range(len(leaves)))
    return jax.tree.map(lambda _: found[next(numbers)], shard)


def entering_2(shard, axes, combine, identity):
    before = start = neutral_like(shard, identity)
    subtotal = shard
    for axis in reversed(axes):
        count, here = (lax.axis_size(axis), lax.axis_index(axis))
        pieces = gathered_once(subtotal, axis)
        inside, subtotal = (start, start)
        for k in range(count):
            passed = k < here
            subtotal = combine(subtotal, jax.tree.map(lambda part: part[k], pieces))
            inside = jax.tree.map(lambda new, old: jnp.where(passed, new, old), subtotal, inside)
        before = combine(inside, before)
    return before


def combine_charge(earlier, later):
    return (earlier[0] * later[0], later[0] * earlier[1] + later[1])


def per_device(
    ptdf,
    demand,
    generation,
    cost,
    gen_cap,
    storage,
    wear,
    initial_charge,
    leakage,
    line_dual,
    line_index,
    rating,
    storage_bus,
    balance_dual,
    hour_block,
    block_price,
):
    limit = jnp.take(rating, line_index)[:, None]
    gathered_units = gather_directly(storage.astype(jnp.bfloat16), "net", 0)
    unit_columns = jnp.take(ptdf, storage_bus, axis=1)
    unit_flow = jnp.dot(unit_columns, gathered_units, preferred_element_type=jnp.float32)
    unit_part = jnp.sum(storage, axis=0)
    dual = line_dual
    price = balance_dual
    rows = generation.shape[0]
    hours = storage.shape[1]
    gen = generation
    buses = rows * lax.axis_size("net")
    for turn in range(PASSES):
        injection = (gen - demand).astype(jnp.bfloat16)
        flows = unit_flow + jnp.dot(
            ptdf, gather_directly(injection, "net", 0), preferred_element_type=jnp.float32
        )
        shifted = flows + dual
        dual = shifted - jnp.clip(shifted, -limit, limit)
        dual_half = dual.astype(jnp.bfloat16)
        pull = summed_on_arrival(
            lax.dot_general(
                ptdf, dual_half, (((0,), (0,)), ((), ())), preferred_element_type=jnp.float32
            ).astype(jnp.bfloat16),
            "net",
            0,
        )
        trial = jnp.clip(gen - STEP * (cost - price[None, :] + pull), 0.0, gen_cap[:, None])
        bus_sum, unit_total = in_one((jnp.sum(trial - demand, axis=0), unit_part), "net")
        mismatch = bus_sum + unit_total
        gen = trial - mismatch[None, :] / buses
        price = price - BAL * mismatch / buses
    blocks = block_price.shape[0]
    hour_price = jnp.sum(
        jnp.where(
            hour_block[:, None] == jnp.arange(blocks, dtype=jnp.int32)[None, :],
            block_price[None, :],
            0.0,
        ),
        axis=1,
    )
    storage_next = jnp.clip(
        storage + STEP_UNIT * (price[None, :] + hour_price[None, :] - wear[:, None] * storage),
        -1.0,
        1.0,
    )
    keep = 1.0 - leakage
    running = -ETA * storage_next
    factor = keep[:, None]
    span = 1
    while span < hours:
        moved = jnp.pad(running[:, :-span], ((0, 0), (span, 0)))
        running = running + factor * moved
        factor = factor * factor
        span = span * 2
    offsets = jnp.arange(1, hours + 1, dtype=jnp.float32)
    growth = jnp.exp(offsets[None, :] * jnp.log(keep)[:, None])
    block_keep = growth[:, -1]
    chained = entering_2(
        (block_keep, running[:, -1]),
        TM,
        combine_charge,
        (jnp.ones_like(block_keep), jnp.zeros_like(block_keep)),
    )
    entering = chained[0] * initial_charge + chained[1]
    charge = growth * entering[:, None] + running
    return (gen, storage_next, charge, dual, price)


def solution(mesh):
    split = Mesh(mesh.devices.reshape(16, 2, mesh.shape["net"]), ("tm_0", "tm_1", "net"))
    in_specs = (
        P("net", None),
        P("net", TM),
        P("net", TM),
        P("net", TM),
        P("net"),
        P("net", TM),
        P("net"),
        P("net"),
        P("net"),
        P("net", TM),
        P("net"),
        P(),
        P(),
        P(TM),
        P(TM),
        P(),
    )
    out_specs = (P("net", TM), P("net", TM), P("net", TM), P("net", TM), P(TM))
    return jax.shard_map(
        per_device, mesh=split, in_specs=in_specs, out_specs=out_specs, check_vma=False
    )
```

profile of v0, /device:TPU:8, one launch (start us, length us, event | category | flops | bytes accessed | tf_op | source)
XLA Modules:
  0.0 187.1 jit_solution(6091052863593614300)
XLA Ops:
  0.6 0.0 copy-start
  0.6 0.9 fusion.42
  1.6 0.8 broadcast_in_dim.72
  2.4 9.1 %all-to-all-start = ((bf16[16,128,64]{1,2,0:T(8,128)(2,1)}), bf16[16,128,64]{1,2,0:T(8,128)(2,1)S(1)}, u32[]{:S(2)}, u32[]{:S(2)}) async-start(bf16[16,128,64]{1,2,0:T(8,128)(2,1)} %broadcast_in_dim.72), calls=%async_computation | async-start | bytes 524288 | tf_op jit(solution)/shard_map/all_to_all | solution.py:25
  11.5 0.7 fusion.12
  12.2 0.7 fusion.13
  12.9 6.1 %gather_fusion.1 = f32[1024]{0:T(1024)S(1)} fusion(f32[4096]{0:T(1024)S(1)} %copy-done, s32[1024]{0:T(1024)S(1)} %fusion.13), kind=kCustom, calls=%fused_computation.1 | custom fusion | bytes 12288 | tf_op jit(solution)/shard_map/jit(_take)/gather | solution.py:118
  19.0 0.7 fusion.41
  19.7 0.9 subtract_convert_fusion.1
  20.6 0.9 broadcast_in_dim.73
  21.5 7.3 %all-to-all-start.1 = ((bf16[16,256,64]{1,2,0:T(8,128)(2,1)}), bf16[16,256,64]{1,2,0:T(8,128)(2,1)S(1)}, u32[]{:S(2)}, u32[]{:S(2)}) async-start(bf16[16,256,64]{1,2,0:T(8,128)(2,1)} %broadcast_in_dim.73), calls=%async_computation.1 | async-start | bytes 1048576 | tf_op jit(solution)/shard_map/all_to_all | solution.py:25
  28.8 0.7 compare_and_fusion
  29.5 12.0 %copy.44 = bf16[1024,4096]{0,1:T(8,128)(2,1)} copy(bf16[1024,4096]{1,0:T(8,128)(2,1)} %param.16) | data formatting | bytes 16777216 | tf_op args[0]
  41.5 15.4 %gather_fusion = bf16[2048,1024]{1,0:T(8,128)(2,1)} fusion(bf16[1024,4096]{0,1:T(8,128)(2,1)} %copy.44, s32[2048]{0:T(1024)S(1)} %fusion.12), kind=kCustom, calls=%fused_computation | custom fusion | bytes 8396800 | tf_op jit(solution)/shard_map/jit(_take)/gather | solution.py:120
  56.9 2.8 %fusion = f32[1024,64]{0,1:T(8,128)S(1)} fusion(bf16[2048,1024]{1,0:T(8,128)(2,1)} %gather_fusion, pred[2048]{0:T(1024)(128)(4,1)S(1)} %compare_and_fusion, bf16[16,128,64]{1,2,0:T(8,128)(2,1)S(1)} %all-to-all-done), kind=kOutput, calls=%fused_computation.4 | convolution fusion | flops 270532608 | bytes 4720640 | tf_op jit(solution)/shard_map/dot_general | solution.py:121
  59.8 6.1 %minimum_subtract_fusion.1 = f32[1024,64]{0,1:T(8,128)S(1)} fusion(f32[1024,64]{0,1:T(8,128)S(1)} %copy-done.3, f32[1024,64]{0,1:T(8,128)S(1)} %fusion, bf16[4096,64]{0,1:T(8,128)(2,1)S(1)} %bitcast.253, bf16[1024,4096]{1,0:T(8,128)(2,1)} %param.16, f32[1024]{0:T(1024)S(1)} %get-tuple-element.15, f32[1024]{0:T(1024)S(1)} %get-tuple-element.16), kind=kOutput, calls=%fused_computation.21 | convolution fusion | flops 537198592 | bytes 9707520 | tf_op jit(solution)/shard_map/dot_general | solution.py:131
  65.9 0.0 copy-start.4
  65.9 0.0 copy-start.5
  65.9 5.0 %convolution_convert_fusion.1 = bf16[64,4096]{1,0:T(8,128)(2,1)S(1)} fusion(bf16[1024,4096]{1,0:T(8,128)(2,1)} %param.16, f32[1024,64]{0,1:T(8,128)S(1)} %minimum_subtract_fusion.1), kind=kOutput, calls=%fused_computation.3 | convolution fusion | flops 537198592 | bytes 9175040 | tf_op jit(solution)/shard_map/dot_general | solution.py:138
  71.0 15.0 %all_to_all.37 = bf16[16,256,64]{1,2,0:T(8,128)(2,1)S(1)} all-to-all(bf16[16,256,64]{1,2,0:T(8,128)(2,1)S(1)} %bitcast.257), channel_id=1, replica_groups=mesh['tm_0'=16,'tm_1'=2,'net'=16] {'net'}, dimensions={0} | all-to-all | bytes 1048576 | tf_op jit(solution)/shard_map/all_to_all | solution.py:40
  86.1 0.1 convert_reduce_fusion.1
  86.2 0.2 subtract_reduce_fusion.1
  86.4 0.1 pad_maximum_fusion
  86.5 11.3 %all_to_all.38 = f32[16,1,128]{2,1,0:T(1,128)S(1)} all-to-all(f32[16,1,128]{2,1,0:T(1,128)S(1)} %broadcast_in_dim.76), channel_id=1, replica_groups=mesh['tm_0'=16,'tm_1'=2,'net'=16] {'net'}, dimensions={0} | all-to-all | bytes 16384 | tf_op jit(solution)/shard_map/all_to_all | solution.py:25
  97.8 0.1 multiply_subtract_fusion.1
  97.9 0.1 subtract_convert_fusion
  98.0 12.4 %all_to_all.39 = bf16[16,256,64]{1,2,0:T(8,128)(2,1)S(1)} all-to-all(bf16[16,256,64]{1,2,0:T(8,128)(2,1)S(1)} %broadcast_in_dim.77), channel_id=1, replica_groups=mesh['tm_0'=16,'tm_1'=2,'net'=16] {'net'}, dimensions={0} | all-to-all | bytes 1048576 | tf_op jit(solution)/shard_map/all_to_all | solution.py:25
  110.4 6.1 %minimum_subtract_fusion = f32[1024,64]{0,1:T(8,128)S(1)} fusion(f32[1024,64]{0,1:T(8,128)S(1)} %minimum_subtract_fusion.1, f32[1024,64]{0,1:T(8,128)S(1)} %fusion, bf16[4096,64]{0,1:T(8,128)(2,1)S(1)} %bitcast.252, bf16[1024,4096]{1,0:T(8,128)(2,1)} %param.16, f32[1024]{0:T(1024)S(1)} %get-tuple-element.15, f32[1024]{0:T(1024)S(1)} %get-tuple-element.16), kind=kOutput, calls=%fused_computation.20 | convolution fusion | flops 537198592 | bytes 9707520 | tf_op jit(solution)/shard_map/dot_general | solution.py:131
  116.5 0.0 copy-start.1
  116.6 5.1 %convolution_convert_fusion = bf16[64,4096]{1,0:T(8,128)(2,1)S(1)} fusion(bf16[1024,4096]{1,0:T(8,128)(2,1)} %param.16, f32[1024,64]{0,1:T(8,128)S(1)} %minimum_subtract_fusion), kind=kOutput, calls=%fused_computation.2 | convolution fusion | flops 537198592 | bytes 9175040 | tf_op jit(solution)/shard_map/dot_general | solution.py:138
  121.6 0.9 copy.63
  122.5 5.6 %all-to-all-start.5 = ((bf16[16,256,64]{1,2,0:T(8,128)(2,1)}), bf16[16,256,64]{1,2,0:T(8,128)(2,1)S(1)}, u32[]{:S(2)}, u32[]{:S(2)}) async-start(bf16[16,256,64]{1,2,0:T(8,128)(2,1)} %bitcast.247), calls=%async_computation.5 | async-start | bytes 1048576 | tf_op jit(solution)/shard_map/all_to_all | solution.py:40
  128.1 0.1 select_reduce_fusion
  128.2 7.9 %all-to-all-done.5 = bf16[16,256,64]{1,2,0:T(8,128)(2,1)S(1)} async-done(((bf16[16,256,64]{1,2,0:T(8,128)(2,1)}), bf16[16,256,64]{1,2,0:T(8,128)(2,1)S(1)}, u32[]{:S(2)}, u32[]{:S(2)}) %all-to-all-start.5) | async-done | bytes 524320 | tf_op jit(solution)/shard_map/all_to_all | solution.py:40
  136.1 0.1 convert_reduce_fusion
  136.2 0.2 subtract_reduce_fusion
  136.4 0.1 pad_maximum_fusion.1
  136.5 0.6 broadcast_in_dim.78
  137.1 5.5 %all-to-all-start.6 = ((f32[16,1,128]{2,1,0:T(1,128)}), f32[16,1,128]{2,1,0:T(1,128)S(1)}, u32[]{:S(2)}, u32[]{:S(2)}) async-start(f32[16,1,128]{2,1,0:T(1,128)} %broadcast_in_dim.78), calls=%async_computation.6 | async-start | bytes 16384 | tf_op jit(solution)/shard_map/all_to_all | solution.py:25
  142.7 6.1 %all-to-all-done.6 = f32[16,1,128]{2,1,0:T(1,128)S(1)} async-done(((f32[16,1,128]{2,1,0:T(1,128)}), f32[16,1,128]{2,1,0:T(1,128)S(1)}, u32[]{:S(2)}, u32[]{:S(2)}) %all-to-all-start.6) | async-done | bytes 8224 | tf_op jit(solution)/shard_map/all_to_all | solution.py:25
  148.9 0.6 fusion.40
  149.5 0.1 broadcast_multiply_fusion
  149.5 0.0 copy-start.6
  149.7 0.1 multiply_add_fusion.1
  149.8 1.8 all-gather.2
  151.6 34.0 %all-gather.3 = f32[16,2,128]{2,1,0:T(2,128)S(1)} all-gather(f32[1,2,128]{2,1,0:T(2,128)S(1)} %maximum_bitcast_fusion.1), channel_id=3, replica_groups=mesh['tm_0'=16,'tm_1'=2,'net'=16] {'tm_0'}, dimensions={0}, use_global_device_ids=true | all-gather | bytes 17408 | tf_op jit(solution)/shard_map/all_gather | solution.py:72
  185.6 0.7 multiply_add_fusion
  186.3 0.7 broadcast_subtract_fusion
  (51 shorter events, 0.4 us)
Async XLA Ops:
  0.6 12.3 %copy-start = (f32[4096]{0:T(1024)S(1)}, f32[4096]{0:T(1024)}, u32[]{:S(2)}) copy-start(f32[4096]{0:T(1024)} %param.27) | copy-start | bytes 49156
  2.4 18.3 %all-to-all-start = ((bf16[16,128,64]{1,2,0:T(8,128)(2,1)}), bf16[16,128,64]{1,2,0:T(8,128)(2,1)S(1)}, u32[]{:S(2)}, u32[]{:S(2)}) async-start(bf16[16,128,64]{1,2,0:T(8,128)(2,1)} %broadcast_in_dim.72), calls=%async_computation | async-start | bytes 524288 | tf_op jit(solution)/shard_map/all_to_all | solution.py:25
  21.5 38.3 %all-to-all-start.1 = ((bf16[16,256,64]{1,2,0:T(8,128)(2,1)}), bf16[16,256,64]{1,2,0:T(8,128)(2,1)S(1)}, u32[]{:S(2)}, u32[]{:S(2)}) async-start(bf16[16,256,64]{1,2,0:T(8,128)(2,1)} %broadcast_in_dim.73), calls=%async_computation.1 | async-start | bytes 1048576 | tf_op jit(solution)/shard_map/all_to_all | solution.py:25
  56.9 2.9 %copy-start.3 = (f32[1024,64]{0,1:T(8,128)S(1)}, f32[1024,64]{0,1:T(8,128)}, u32[]{:S(2)}) copy-start(f32[1024,64]{0,1:T(8,128)} %param.25) | copy-start | bytes 786436
  65.9 20.2 %copy-start.2 = (f32[256,64]{0,1:T(8,128)S(1)}, f32[256,64]{0,1:T(8,128)}, u32[]{:S(2)}) copy-start(f32[256,64]{0,1:T(8,128)} %param.17) | copy-start | bytes 196612
  65.9 20.2 %copy-start.4 = (f32[256,64]{0,1:T(8,128)S(1)}, f32[256,64]{0,1:T(8,128)}, u32[]{:S(2)}) copy-start(f32[256,64]{0,1:T(8,128)} %param.19) | copy-start | bytes 196612
  65.9 20.2 %copy-start.5 = (f32[256,64]{0,1:T(8,128)S(1)}, f32[256,64]{0,1:T(8,128)}, u32[]{:S(2)}) copy-start(f32[256,64]{0,1:T(8,128)} %param.18) | copy-start | bytes 196612
  65.9 20.2 %copy-start.8 = (f32[256]{0:T(256)S(1)}, f32[256]{0:T(256)}, u32[]{:S(2)}) copy-start(f32[256]{0:T(256)} %param.20) | copy-start | bytes 3076
  65.9 20.2 %copy-start.9 = (f32[64]{0:T(128)S(1)}, f32[64]{0:T(128)}, u32[]{:S(2)}) copy-start(f32[64]{0:T(128)} %param.29) | copy-start | bytes 772
  116.5 6.0 %copy-start.1 = (f32[1024,64]{0,1:T(8,128)}, f32[1024,64]{0,1:T(8,128)S(1)}, u32[]{:S(2)}) copy-start(f32[1024,64]{0,1:T(8,128)S(1)} %minimum_subtract_fusion) | copy-start | bytes 786436
  116.5 11.6 %copy-start.13 = (f32[24]{0:T(128)S(1)}, f32[24]{0:T(128)}, u32[]{:S(2)}) copy-start(f32[24]{0:T(128)} %param.31) | copy-start | bytes 292
  116.5 11.6 %copy-start.14 = (s32[64]{0:T(128)S(1)}, s32[64]{0:T(128)}, u32[]{:S(2)}) copy-start(s32[64]{0:T(128)} %param.30) | copy-start | bytes 772
  116.5 11.7 %copy-start.12 = (f32[128]{0:T(128)S(1)}, f32[128]{0:T(128)}, u32[]{:S(2)}) copy-start(f32[128]{0:T(128)} %param.24) | copy-start | bytes 1540
  116.5 32.9 %copy-start.7 = (f32[128,64]{0,1:T(8,128)S(1)}, f32[128,64]{0,1:T(8,128)}, u32[]{:S(2)}) copy-start(f32[128,64]{0,1:T(8,128)} %param.21) | copy-start | bytes 98308
  116.5 32.9 %copy-start.10 = (f32[128]{0:T(128)S(1)}, f32[128]{0:T(128)}, u32[]{:S(2)}) copy-start(f32[128]{0:T(128)} %param.22) | copy-start | bytes 1540
  116.5 69.0 %copy-start.11 = (f32[128]{0:T(128)S(1)}, f32[128]{0:T(128)}, u32[]{:S(2)}) copy-start(f32[128]{0:T(128)} %param.23) | copy-start | bytes 1540
  122.5 13.7 %all-to-all-start.5 = ((bf16[16,256,64]{1,2,0:T(8,128)(2,1)}), bf16[16,256,64]{1,2,0:T(8,128)(2,1)S(1)}, u32[]{:S(2)}, u32[]{:S(2)}) async-start(bf16[16,256,64]{1,2,0:T(8,128)(2,1)} %bitcast.247), calls=%async_computation.5 | async-start | bytes 1048576 | tf_op jit(solution)/shard_map/all_to_all | solution.py:40
  137.1 11.8 %all-to-all-start.6 = ((f32[16,1,128]{2,1,0:T(1,128)}), f32[16,1,128]{2,1,0:T(1,128)S(1)}, u32[]{:S(2)}, u32[]{:S(2)}) async-start(f32[16,1,128]{2,1,0:T(1,128)} %broadcast_in_dim.78), calls=%async_computation.6 | async-start | bytes 16384 | tf_op jit(solution)/shard_map/all_to_all | solution.py:25
  149.5 37.5 %copy-start.6 = (f32[128,64]{0,1:T(8,128)}, f32[128,64]{0,1:T(8,128)S(1)}, u32[]{:S(2)}) copy-start(f32[128,64]{0,1:T(8,128)S(1)} %get-tuple-element.8) | copy-start | bytes 98308
where the time goes:
time: 188 us; the launch traced here: 187 us
  blocking collectives  74.5 us (40%)
  local copies, waits for them, and re-layouts  37 us (20%)
  starting transfers between devices  27.5 us (15%)
  matrix products  25.1 us (13%)
  waiting for transfers between devices  14.1 us (8%)
  other arithmetic  7.88 us (4%)
    all_gather x2, blocking collectives, gathered_once(): both, at, found = (lax.all_gather(jnp.concatenate(lines), axis), 0, {})  35.8 us
    all_to_all x2, blocking collectives, sent_to_all(): return lax.all_to_all(copies, axis, split_axis=0, concat_axis=0, tiled=True)  23.7 us
    all_to_all x3, starting transfers between devices, sent_to_all(): return lax.all_to_all(copies, axis, split_axis=0, concat_axis=0, tiled=True)  21.9 us
    gather x1, local copies, waits for them, and re-layouts, per_device(): unit_columns = jnp.take(ptdf, storage_bus, axis=1)  15.4 us
    all_to_all x1, blocking collectives, summed_on_arrival(): lax.all_to_all(parts, axis, split_axis=0, concat_axis=0, tiled=True)  15 us
    dot_general x2, matrix products, per_device(): jnp.dot(ptdf, gather_directly(injection, 'net', 0), preferred_element_typ...  12.1 us
    unnamed x31, local copies, waits for them, and re-layouts  12.1 us
    dot_general x2, matrix products, per_device(): lax.dot_general(ptdf, dual_half, (((0,), (0,)), ((), ())), preferred_elem...  10.1 us
  transfers between devices with their start and end apart: 4, of which 2 were waited for; matrix products, arithmetic and copies ran while one was open for 21% of the time, Pallas kernels for 0%

commit v1 on v0

v1 whole, which is shorter than its diff:
```python
import jax
import jax.numpy as jnp
from jax import lax
from jax.experimental import pallas as pl
from jax.experimental.pallas import tpu as pltpu
from jax.sharding import Mesh
from jax.sharding import PartitionSpec as P

TM = ("tm_0", "tm_1")

STEP = 0.1
BAL = 0.5
STEP_UNIT = 0.2
ETA = 0.0625

F32 = jnp.float32
BF16 = jnp.bfloat16
NT = (((1,), (1,)), ((), ()))


def call(kernel, name, *outs):
    return pl.pallas_call(
        kernel,
        name=name,
        out_shape=tuple(jax.ShapeDtypeStruct(s, d) for s, d in outs),
        compiler_params=pltpu.CompilerParams(vmem_limit_bytes=48 << 20),
    )


def shape(s, d):
    return s, d


def iota(dims, axis):
    return lax.broadcasted_iota(jnp.int32, dims, axis)


def column(row, n):
    eye = iota((n, n), 0) == iota((n, n), 1)
    return jnp.sum(jnp.where(eye, row[:, :n], jnp.zeros((), row.dtype)), axis=1, keepdims=True)


def row_of(col, width):
    n = col.shape[0]
    eye = iota((n, width), 0) == iota((n, width), 1)
    return jnp.sum(jnp.where(eye, col, 0.0), axis=0, keepdims=True)


def three_parts(value):
    high = value.astype(BF16)
    rest = value - high.astype(F32)
    middle = rest.astype(BF16)
    low = (rest - middle.astype(F32)).astype(BF16)
    return high, middle, low


def pack_body(gen, demand, storage, out):
    rows = gen.shape[1]
    injection = (gen[...] - demand[...]).astype(BF16)
    units = storage[...].astype(BF16)
    for d in range(out.shape[0]):
        out[d, :, :rows] = injection
        out[d, :, rows:] = units


def tables_body(rating, index, leakage, hour_block, block_price, limit, growth, hour_price):
    groups = rating.shape[0]
    at = index[...]
    hot = (iota((groups, at.shape[1]), 0) == at // 128).astype(BF16)
    table = rating[...].T
    picked = sum(jnp.dot(part, hot, preferred_element_type=F32) for part in three_parts(table))
    here = iota((128, at.shape[1]), 0) == at % 128
    limit[...] = jnp.sum(jnp.where(here, picked, 0.0), axis=0, keepdims=True)
    hours, units = growth.shape
    offsets = (iota((hours, units), 0) + 1).astype(F32)
    growth[...] = jnp.exp(offsets * jnp.log(1.0 - leakage[...]))
    block = column(hour_block[...], hours)
    blocks = block_price.shape[1]
    price = jnp.where(block == iota((hours, blocks), 1), block_price[...], 0.0)
    hour_price[...] = jnp.broadcast_to(jnp.sum(price, axis=1, keepdims=True), hour_price.shape)


def clipped(flows, dual, limit):
    shifted = flows + dual
    return shifted - jnp.clip(shifted, -limit, limit)


def pull_parts(dual, ptdf, out):
    pull = jnp.dot(dual.astype(BF16), ptdf[...], preferred_element_type=F32)
    rows = out.shape[2]
    for d in range(out.shape[0]):
        out[d] = pull[:, d * rows : (d + 1) * rows].astype(BF16)


def first_body(arrived, ptdf, line_dual, limit, bus, parts, dual_out, unit_flow_out):
    count, hours, width = arrived.shape
    rows = parts.shape[2]
    units = width - rows
    spread = jnp.zeros((count * hours, rows), F32)
    for k in range(0, count, 2):
        at = bus[:, k * units : (k + 2) * units]
        owner, place = at // rows, at % rows
        storage = jnp.concatenate([arrived[k, :, rows:], arrived[k + 1, :, rows:]], axis=1)
        hot = (iota((rows, 2 * units), 0) == place).astype(F32).astype(BF16)
        owned = [
            storage * jnp.broadcast_to((owner == d).astype(F32), storage.shape).astype(BF16)
            for d in range(count)
        ]
        spread += lax.dot_general(
            jnp.concatenate(owned, axis=0), hot, NT, preferred_element_type=F32
        )
    lefts = []
    for d in range(count):
        part = spread[d * hours : (d + 1) * hours]
        high = part.astype(BF16)
        low = (part - high.astype(F32)).astype(BF16)
        lefts.append(jnp.concatenate([arrived[d, :, :rows], high, low], axis=0))
    products = lax.dot_general(
        jnp.concatenate(lefts, axis=1), ptdf[...], NT, preferred_element_type=F32
    )
    unit_flow = products[hours : 2 * hours] + products[2 * hours :]
    unit_flow_out[...] = unit_flow
    dual = clipped(products[:hours] + unit_flow, line_dual[...], limit[...])
    dual_out[...] = dual
    pull_parts(dual, ptdf, parts)


def second_body(arrived, ptdf, line_dual, limit, unit_flow, parts, dual_out, mean_out):
    count, rows = parts.shape[0], parts.shape[2]
    hours = parts.shape[1]
    total = arrived[0, :hours]
    extra = arrived[0, hours : hours + 1]
    for d in range(1, count):
        total += arrived[d, :hours]
        extra += arrived[d, hours : hours + 1]
    mismatch = jnp.sum(total, axis=1, keepdims=True) + column(extra, hours)
    mean = mismatch / (count * rows)
    mean_out[...] = jnp.broadcast_to(mean, mean_out.shape)
    injection = [(arrived[d, :hours] - mean).astype(BF16) for d in range(count)]
    flows = lax.dot_general(
        jnp.concatenate(injection, axis=1), ptdf[...], NT, preferred_element_type=F32
    )
    dual = clipped(flows + unit_flow[...], line_dual[...], limit[...])
    dual_out[...] = dual
    pull_parts(dual, ptdf, parts)


def total_of(arrived):
    total = arrived[0].astype(F32)
    for d in range(1, arrived.shape[0]):
        total += arrived[d].astype(F32)
    return total


def trial_body(arrived, gen, cost, demand, price, cap, storage, send, trial_out):
    hours = gen.shape[0]
    pull = total_of(arrived)
    now = column(price[...], hours)
    trial = jnp.clip(gen[...] - STEP * (cost[...] - now + pull), 0.0, cap[...])
    trial_out[...] = trial
    balance = trial - demand[...]
    unit_sum = row_of(jnp.sum(storage[...], axis=1, keepdims=True), send.shape[2])
    below = jnp.broadcast_to(unit_sum, (send.shape[1] - hours, send.shape[2]))
    for d in range(send.shape[0]):
        send[d, :hours] = balance
        send[d, hours:] = below


def last_trial_body(arrived, before, mean, cost, demand, price, cap, storage, send, trial_out):
    hours = before.shape[0]
    pull = total_of(arrived)
    moved = mean[:, :1]
    now = column(price[...], hours) - BAL * moved
    trial = jnp.clip(before[...] - moved - STEP * (cost[...] - now + pull), 0.0, cap[...])
    trial_out[...] = trial
    own = jnp.sum(trial - demand[...], axis=1, keepdims=True)
    own += jnp.sum(storage[...], axis=1, keepdims=True)
    send[...] = jnp.broadcast_to(row_of(own, send.shape[2])[None], send.shape)


def finish_body(
    arrived, trial, mean, price, hour_price, storage, wear, growth, gen_out, storage_out, running_out, price_out, last_out
):
    hours, units = storage.shape
    buses = arrived.shape[0] * trial.shape[1]
    mismatch = column(total_of(arrived)[:1], hours) / buses
    gen_out[...] = trial[...] - mismatch
    now = column(price[...], hours) - BAL * mean[:, :1] - BAL * mismatch
    price_out[...] = row_of(now, price_out.shape[1])
    held = storage[...]
    nexts = jnp.clip(held + STEP_UNIT * (now + hour_price[...] - wear[...] * held), -1.0, 1.0)
    storage_out[...] = nexts
    running = -ETA * nexts
    hour = iota((hours, units), 0)
    span = 1
    while span < hours:
        moved = jnp.where(hour >= span, pltpu.roll(running, span, 0), 0.0)
        running = running + growth[span - 1 : span] * moved
        span *= 2
    running_out[...] = running
    last_out[...] = jnp.broadcast_to(running[hours - 1 :], last_out.shape)


def chip_body(pair, growth, send):
    hours = growth.shape[0]
    both = growth[hours - 1 :] * pair[0] + pair[1]
    send[...] = jnp.broadcast_to(both[None], send.shape)


def charge_body(here, arrived, pair, growth, initial, running, charge):
    hours = growth.shape[0]
    keep = growth[hours - 1 :]
    twice = keep * keep
    entering = initial[...]
    for k in range(arrived.shape[0]):
        entering = jnp.where(k < here[0], twice * entering + arrived[k, :1], entering)
    entering = jnp.where(here[1] > 0, keep * entering + pair[0, :1], entering)
    charge[...] = growth[...] * entering + running[...]


def everywhere(blocks, axis):
    return lax.all_to_all(blocks, axis, split_axis=0, concat_axis=0, tiled=True)


def per_device(
    ptdf,
    demand,
    generation,
    cost,
    gen_cap,
    storage,
    wear,
    initial_charge,
    leakage,
    line_dual,
    line_index,
    rating,
    storage_bus,
    balance_dual,
    hour_block,
    block_price,
):
    net = lax.axis_size("net")
    chips = lax.axis_size("tm_0")
    lines = ptdf.shape[0]
    rows, hours = generation.shape
    units = storage.shape[0]
    demand, gen, cost, held = demand.T, generation.T, cost.T, storage.T
    dual = line_dual.T
    cap, wear, initial = gen_cap[None], wear[None], initial_charge[None]
    price = balance_dual[None]
    (packed,) = call(pack_body, "pack", shape((net, hours, rows + units), BF16))(gen, demand, held)
    arrived = everywhere(packed, "net")
    limit, growth, hour_price = call(
        tables_body,
        "tables",
        shape((1, lines), F32),
        shape((hours, units), F32),
        shape((hours, units), F32),
    )(rating.reshape(-1, 128), line_index[None], leakage[None], hour_block[None], block_price[None])
    parts, dual, unit_flow = call(
        first_body,
        "first",
        shape((net, hours, rows), BF16),
        shape((hours, lines), F32),
        shape((hours, lines), F32),
    )(arrived, ptdf, dual, limit, storage_bus[None])
    arrived = everywhere(parts, "net")
    send, trial = call(
        trial_body, "trial", shape((net, hours + 8, rows), F32), shape((hours, rows), F32)
    )(arrived, gen, cost, demand, price, cap, held)
    arrived = everywhere(send, "net")
    parts, dual, mean = call(
        second_body,
        "second",
        shape((net, hours, rows), BF16),
        shape((hours, lines), F32),
        shape((hours, 128), F32),
    )(arrived, ptdf, dual, limit, unit_flow)
    arrived = everywhere(parts, "net")
    send, trial = call(
        last_trial_body, "last_trial", shape((net, 8, 128), F32), shape((hours, rows), F32)
    )(arrived, trial, mean, cost, demand, price, cap, held)
    arrived = everywhere(send, "net")
    gen, storage_next, running, price, last = call(
        finish_body,
        "finish",
        shape((hours, rows), F32),
        shape((hours, units), F32),
        shape((hours, units), F32),
        shape((1, hours), F32),
        shape((8, units), F32),
    )(arrived, trial, mean, price, hour_price, held, wear, growth)
    pair = lax.all_gather(last, "tm_1")
    (send,) = call(chip_body, "chip", shape((chips, 8, units), F32))(pair, growth)
    arrived = everywhere(send, "tm_0")
    here = jnp.stack([lax.axis_index("tm_0"), lax.axis_index("tm_1")])
    smem = pl.BlockSpec(memory_space=pltpu.SMEM)
    vmem = pl.BlockSpec(memory_space=pltpu.VMEM)
    charge = pl.pallas_call(
        charge_body,
        name="charge",
        in_specs=[smem] + [vmem] * 5,
        out_shape=jax.ShapeDtypeStruct((hours, units), F32),
    )(here, arrived, pair, growth, initial, running)
    return (gen.T, storage_next.T, charge.T, dual.T, price[0])


def solution(mesh):
    split = Mesh(mesh.devices.reshape(16, 2, mesh.shape["net"]), ("tm_0", "tm_1", "net"))
    in_specs = (
        P("net", None),
        P("net", TM),
        P("net", TM),
        P("net", TM),
        P("net"),
        P("net", TM),
        P("net"),
        P("net"),
        P("net"),
        P("net", TM),
        P("net"),
        P(),
        P(),
        P(TM),
        P(TM),
        P(),
    )
    out_specs = (P("net", TM), P("net", TM), P("net", TM), P("net", TM), P(TM))
    return jax.shard_map(
        per_device, mesh=split, in_specs=in_specs, out_specs=out_specs, check_vma=False
    )
```

time: 188 us -> 137 us (0.73)
  the two profiles are of different devices: /device:TPU:8 before, /device:TPU:1 now
where the time goes in v1:
time: 137 us; the launch traced here: 136 us
  blocking collectives  59.8 us (44%)
  starting transfers between devices  25.9 us (19%)
  Pallas kernels  22.9 us (17%)
  waiting for transfers between devices  22.3 us (16%)
  local copies, waits for them, and re-layouts  3.74 us (3%)
    all_to_all x4, blocking collectives, everywhere(): return lax.all_to_all(blocks, axis, split_axis=0, concat_axis=0, tiled=True)  49.8 us
    all_to_all x2, starting transfers between devices, everywhere(): return lax.all_to_all(blocks, axis, split_axis=0, concat_axis=0, tiled=True)  25.9 us
    all_to_all x2, waiting for transfers between devices, everywhere(): return lax.all_to_all(blocks, axis, split_axis=0, concat_axis=0, tiled=True)  22.3 us
    pallas_call x1, Pallas kernels, per_device(): call(first_body, 'first', shape((net, hours, rows), BF16), shape((hours,...  10.4 us
    all_gather x1, blocking collectives, per_device(): pair = lax.all_gather(last, 'tm_1')  10 us
    pallas_call x1, Pallas kernels, per_device(): call(second_body, 'second', shape((net, hours, rows), BF16), shape((hours...  7.58 us
    unnamed x42, local copies, waits for them, and re-layouts  3.74 us
  transfers between devices with their start and end apart: 2, of which 2 were waited for; matrix products, arithmetic and copies ran while one was open for 0% of the time, Pallas kernels for 0%

profile of v1, /device:TPU:1, one launch (start us, length us, event | category | flops | bytes accessed | tf_op | source)
XLA Modules:
  0.0 136.2 jit_solution(17145071167735344383)
XLA Ops:
  0.6 0.0 copy-start
  0.6 0.8 copy-done
  1.5 0.8 copy-done.2
  2.2 0.8 copy-done.7
  3.1 0.0 copy-start.19
  3.1 0.0 copy-start.5
  3.1 0.0 copy-start.12
  3.1 1.0 pack.1
  4.1 7.6 %all-to-all-start = ((bf16[16,64,384]{2,1,0:T(8,128)(2,1)}), bf16[16,64,384]{2,1,0:T(8,128)(2,1)S(1)}, u32[]{:S(2)}, u32[]{:S(2)}) async-start(bf16[16,64,384]{2,1,0:T(8,128)(2,1)} %pack.1), calls=%async_computation | async-start | bytes 1572864 | tf_op jit(solution)/shard_map/all_to_all | solution.py:222
  11.7 0.0 copy-done.11
  11.7 0.0 copy-done.15
  11.7 0.0 copy-done.17
  11.7 0.0 copy-done.18
  11.8 0.0 copy-done.19
  11.8 0.4 tables.1
  12.2 0.0 copy-start.4
  12.2 11.3 %all-to-all-done.arrived = bf16[16,64,384]{2,1,0:T(8,128)(2,1)S(1)} async-done(((bf16[16,64,384]{2,1,0:T(8,128)(2,1)}), bf16[16,64,384]{2,1,0:T(8,128)(2,1)S(1)}, u32[]{:S(2)}, u32[]{:S(2)}) %all-to-all-start) | async-done | bytes 786464 | tf_op jit(solution)/shard_map/all_to_all | solution.py:222
  23.5 0.0 copy-done.5
  23.5 0.0 copy-done.12
  23.5 0.0 copy-start.6
  23.5 0.0 copy-start.8
  23.5 0.0 copy-start.13
  23.5 0.0 copy-start.14
  23.6 10.4 %first.1 = (bf16[16,64,256]{2,1,0:T(8,128)(2,1)S(1)}, f32[64,1024]{1,0:T(8,128)S(1)}, f32[64,1024]{1,0:T(8,128)S(1)}) custom-call(bf16[16,64,384]{2,1,0:T(8,128)(2,1)S(1)} %all-to-all-done.arrived, bf16[1024,4096]{1,0:T(8,128)(2,1)} %ptdf.3, f32[64,1024]{1,0:T(8,128)S(1)} %bitcast.30, f32[1,1024]{1,0:T(1,128)S(1)} %get-tuple-element.23.limit, ...), custom_call_target="tpu_custom_call" | custom-call | tf_op jit(solution)/shard_map/first/pallas_call | solution.py:261
  34.0 12.2 %all_to_all.30.arrived = bf16[16,64,256]{2,1,0:T(8,128)(2,1)S(1)} all-to-all(bf16[16,64,256]{2,1,0:T(8,128)(2,1)S(1)} %get-tuple-element.24), channel_id=1, replica_groups=mesh['tm_0'=16,'tm_1'=2,'net'=16] {'net'}, dimensions={0} | all-to-all | bytes 1048576 | tf_op jit(solution)/shard_map/all_to_all | solution.py:222
  46.2 0.0 copy-done.1
  46.2 0.0 copy-done.3
  46.2 0.0 copy-done.6
  46.2 0.0 copy-done.8
  46.2 0.0 copy-done.13
  46.2 0.0 copy-done.14
  46.2 0.2 trial.1
  46.4 16.6 %all_to_all.31.arrived = f32[16,72,256]{2,1,0:T(8,128)S(1)} all-to-all(f32[16,72,256]{2,1,0:T(8,128)S(1)} %get-tuple-element.25), channel_id=1, replica_groups=mesh['tm_0'=16,'tm_1'=2,'net'=16] {'net'}, dimensions={0} | all-to-all | bytes 2359296 | tf_op jit(solution)/shard_map/all_to_all | solution.py:222
  63.0 7.6 %second.1 = (bf16[16,64,256]{2,1,0:T(8,128)(2,1)S(1)}, f32[64,1024]{1,0:T(8,128)}, f32[64,128]{1,0:T(8,128)S(1)}) custom-call(f32[16,72,256]{2,1,0:T(8,128)S(1)} %all_to_all.31.arrived, bf16[1024,4096]{1,0:T(8,128)(2,1)} %ptdf.3, f32[64,1024]{1,0:T(8,128)S(1)} %get-tuple-element.26.line_dual, f32[1,1024]{1,0:T(1,128)S(1)} %get-tuple-element.23.limit, ...), custom_call_target="tpu_custom_call" | custom-call | tf_op jit(solution)/shard_map/second/pallas_call | solution.py:273
  70.6 0.0 copy-start.16
  70.6 11.8 %all_to_all.32.arrived = bf16[16,64,256]{2,1,0:T(8,128)(2,1)S(1)} all-to-all(bf16[16,64,256]{2,1,0:T(8,128)(2,1)S(1)} %get-tuple-element.28), channel_id=1, replica_groups=mesh['tm_0'=16,'tm_1'=2,'net'=16] {'net'}, dimensions={0} | all-to-all | bytes 1048576 | tf_op jit(solution)/shard_map/all_to_all | solution.py:222
  82.4 0.3 last_trial.1
  82.7 9.2 %all_to_all.33.arrived = f32[16,8,128]{2,1,0:T(8,128)S(1)} all-to-all(f32[16,8,128]{2,1,0:T(8,128)S(1)} %get-tuple-element.31), channel_id=1, replica_groups=mesh['tm_0'=16,'tm_1'=2,'net'=16] {'net'}, dimensions={0} | all-to-all | bytes 131072 | tf_op jit(solution)/shard_map/all_to_all | solution.py:222
  91.9 0.0 copy-done.16
  91.9 0.8 finish.1
  92.7 0.6 copy-done.10
  93.3 10.0 %all-gather = f32[16,128]{1,0:T(8,128)S(1)} all-gather(f32[8,128]{1,0:T(8,128)S(1)} %get-tuple-element.37), channel_id=2, replica_groups=mesh['tm_0'=16,'tm_1'=2,'net'=16] {'tm_1'}, dimensions={0}, use_global_device_ids=true | all-gather | bytes 12288 | tf_op jit(solution)/shard_map/all_gather | solution.py:294
  103.3 0.6 chip.1
  104.0 18.3 %all-to-all-start.5 = ((f32[16,8,128]{2,1,0:T(8,128)}), f32[16,8,128]{2,1,0:T(8,128)S(1)}, u32[]{:S(2)}, u32[]{:S(2)}) async-start(f32[16,8,128]{2,1,0:T(8,128)} %chip.1), calls=%async_computation.5 | async-start | bytes 131072 | tf_op jit(solution)/shard_map/all_to_all | solution.py:222
  122.3 0.7 pad_add_fusion.here
  123.0 11.0 %all-to-all-done.5.arrived = f32[16,8,128]{2,1,0:T(8,128)S(1)} async-done(((f32[16,8,128]{2,1,0:T(8,128)}), f32[16,8,128]{2,1,0:T(8,128)S(1)}, u32[]{:S(2)}, u32[]{:S(2)}) %all-to-all-start.5) | async-done | bytes 65568 | tf_op jit(solution)/shard_map/all_to_all | solution.py:222
  134.0 0.6 copy-done.20
  134.6 1.6 %charge.1 = f32[64,128]{1,0:T(8,128)} custom-call(s32[2]{0:T(128)} %pad_add_fusion.here, f32[16,8,128]{2,1,0:T(8,128)} %copy-done.20, f32[2,8,128]{2,1,0:T(8,128)} %bitcast.36, f32[64,128]{1,0:T(8,128)} %copy-done.4, f32[1,128]{1,0:T(1,128)} %bitcast.50, f32[64,128]{1,0:T(8,128)} %copy-done.10), custom_call_target="tpu_custom_call" | custom-call | tf_op jit(solution)/shard_map/charge/pallas_call | solution.py:300
  (13 shorter events, 0.0 us)
Async XLA Ops:
  0.6 0.8 copy-start
  1.5 0.8 copy-start.2
  2.2 0.8 copy-start.7
  3.1 8.6 %copy-start.11 = (f32[4096]{0:T(1024)S(1)}, f32[4096]{0:T(1024)}, u32[]{:S(2)}) copy-start(f32[4096]{0:T(1024)} %param.27) | copy-start | bytes 49156
  3.1 8.7 %copy-start.15 = (s32[1024]{0:T(1024)S(1)}, s32[1024]{0:T(1024)}, u32[]{:S(2)}) copy-start(s32[1024]{0:T(1024)} %param.26) | copy-start | bytes 12292
  3.1 8.7 %copy-start.17 = (f32[128]{0:T(128)S(1)}, f32[128]{0:T(128)}, u32[]{:S(2)}) copy-start(f32[128]{0:T(128)} %param.24) | copy-start | bytes 1540
  3.1 8.7 %copy-start.18 = (s32[64]{0:T(128)S(1)}, s32[64]{0:T(128)}, u32[]{:S(2)}) copy-start(s32[64]{0:T(128)} %param.30) | copy-start | bytes 772
  3.1 8.7 %copy-start.19 = (f32[24]{0:T(128)S(1)}, f32[24]{0:T(128)}, u32[]{:S(2)}) copy-start(f32[24]{0:T(128)} %param.31) | copy-start | bytes 292
  3.1 20.4 %copy-start.5 = (f32[1024,64]{0,1:T(8,128)S(1)}, f32[1024,64]{0,1:T(8,128)}, u32[]{:S(2)}) copy-start(f32[1024,64]{0,1:T(8,128)} %param.25) | copy-start | bytes 786436
  3.1 20.4 %copy-start.12 = (s32[2048]{0:T(1024)S(1)}, s32[2048]{0:T(1024)}, u32[]{:S(2)}) copy-start(s32[2048]{0:T(1024)} %param.28) | copy-start | bytes 24580
  4.1 19.4 %all-to-all-start = ((bf16[16,64,384]{2,1,0:T(8,128)(2,1)}), bf16[16,64,384]{2,1,0:T(8,128)(2,1)S(1)}, u32[]{:S(2)}, u32[]{:S(2)}) async-start(bf16[16,64,384]{2,1,0:T(8,128)(2,1)} %pack.1), calls=%async_computation | async-start | bytes 1572864 | tf_op jit(solution)/shard_map/all_to_all | solution.py:222
  12.2 91.1 %copy-start.4 = (f32[64,128]{1,0:T(8,128)}, f32[64,128]{1,0:T(8,128)S(1)}, u32[]{:S(2)}) copy-start(f32[64,128]{1,0:T(8,128)S(1)} %get-tuple-element.34.growth) | copy-start | bytes 98308
  23.5 22.7 %copy-start.1 = (f32[256,64]{0,1:T(8,128)S(1)}, f32[256,64]{0,1:T(8,128)}, u32[]{:S(2)}) copy-start(f32[256,64]{0,1:T(8,128)} %param.17) | copy-start | bytes 196612
  23.5 22.7 %copy-start.3 = (f32[128,64]{0,1:T(8,128)S(1)}, f32[128,64]{0,1:T(8,128)}, u32[]{:S(2)}) copy-start(f32[128,64]{0,1:T(8,128)} %param.21) | copy-start | bytes 98308
  23.5 22.7 %copy-start.6 = (f32[256,64]{0,1:T(8,128)S(1)}, f32[256,64]{0,1:T(8,128)}, u32[]{:S(2)}) copy-start(f32[256,64]{0,1:T(8,128)} %param.19) | copy-start | bytes 196612
  23.5 22.7 %copy-start.8 = (f32[256,64]{0,1:T(8,128)S(1)}, f32[256,64]{0,1:T(8,128)}, u32[]{:S(2)}) copy-start(f32[256,64]{0,1:T(8,128)} %param.18) | copy-start | bytes 196612
  23.5 22.7 %copy-start.13 = (f32[64]{0:T(128)S(1)}, f32[64]{0:T(128)}, u32[]{:S(2)}) copy-start(f32[64]{0:T(128)} %param.29) | copy-start | bytes 772
  23.5 22.7 %copy-start.14 = (f32[256]{0:T(256)S(1)}, f32[256]{0:T(256)}, u32[]{:S(2)}) copy-start(f32[256]{0:T(256)} %param.20) | copy-start | bytes 3076
  70.6 21.3 %copy-start.16 = (f32[128]{0:T(128)S(1)}, f32[128]{0:T(128)}, u32[]{:S(2)}) copy-start(f32[128]{0:T(128)} %param.22) | copy-start | bytes 1540
  92.7 0.6 copy-start.10
  103.3 30.7 %copy-start.9 = (f32[16,128]{1,0:T(8,128)}, f32[16,128]{1,0:T(8,128)S(1)}, u32[]{:S(2)}) copy-start(f32[16,128]{1,0:T(8,128)S(1)} %all-gather) | copy-start | bytes 24580
  104.0 30.0 %all-to-all-start.5 = ((f32[16,8,128]{2,1,0:T(8,128)}), f32[16,8,128]{2,1,0:T(8,128)S(1)}, u32[]{:S(2)}, u32[]{:S(2)}) async-start(f32[16,8,128]{2,1,0:T(8,128)} %chip.1), calls=%async_computation.5 | async-start | bytes 131072 | tf_op jit(solution)/shard_map/all_to_all | solution.py:222
  134.0 0.6 copy-start.20

commit v2 on v1

--- a/solution.py
+++ b/solution.py
@@ -14,6 +14,8 @@
 ETA = 0.0625
 
 F32 = jnp.float32
+VMEM_LIMIT = 16 << 20
+CHUNKS = 4
 BF16 = jnp.bfloat16
 NT = (((1,), (1,)), ((), ()))
 
@@ -23,7 +25,7 @@
         kernel,
         name=name,
         out_shape=tuple(jax.ShapeDtypeStruct(s, d) for s, d in outs),
-        compiler_params=pltpu.CompilerParams(vmem_limit_bytes=48 << 20),
+        compiler_params=pltpu.CompilerParams(vmem_limit_bytes=VMEM_LIMIT),
     )
 
 
@@ -54,7 +56,13 @@
     return high, middle, low
 
 
-def pack_body(gen, demand, storage, out):
+def pack_body(gen_in, demand_in, storage_in, out, gen, demand, storage, sems):
+    pairs = ((gen_in, gen), (demand_in, demand), (storage_in, storage))
+    copies = [pltpu.make_async_copy(a, b, sems.at[k]) for k, (a, b) in enumerate(pairs)]
+    for copy in copies:
+        copy.start()
+    for copy in copies:
+        copy.wait()
     rows = gen.shape[1]
     injection = (gen[...] - demand[...]).astype(BF16)
     units = storage[...].astype(BF16)
@@ -63,17 +71,27 @@
         out[d, :, rows:] = units
 
 
-def tables_body(rating, index, leakage, hour_block, block_price, limit, growth, hour_price):
+def write_tables(
+    here, rating, index, leakage, hour_block, block_price, initial, limit, growth, hour_price, chain
+):
     groups = rating.shape[0]
     at = index[...]
     hot = (iota((groups, at.shape[1]), 0) == at // 128).astype(BF16)
     table = rating[...].T
     picked = sum(jnp.dot(part, hot, preferred_element_type=F32) for part in three_parts(table))
-    here = iota((128, at.shape[1]), 0) == at % 128
-    limit[...] = jnp.sum(jnp.where(here, picked, 0.0), axis=0, keepdims=True)
+    found = iota((128, at.shape[1]), 0) == at % 128
+    limit[...] = jnp.sum(jnp.where(found, picked, 0.0), axis=0, keepdims=True)
     hours, units = growth.shape
     offsets = (iota((hours, units), 0) + 1).astype(F32)
-    growth[...] = jnp.exp(offsets * jnp.log(1.0 - leakage[...]))
+    rate = jnp.log(1.0 - leakage[...])
+    growth[...] = jnp.exp(offsets * rate)
+    count = chain.shape[0] - 8
+    row = iota(chain.shape, 0)
+    spans = jnp.where(row < count, 2 * (here[0] - 1 - row), 2 * here[0]) + here[1]
+    weight = jnp.exp((jnp.maximum(spans, 0) * hours).astype(F32) * rate)
+    weight = jnp.where((row < here[0]) | (row == count), weight, 0.0)
+    weight = jnp.where(row == count, weight * initial[...], weight)
+    chain[...] = jnp.where(row == count + 1, here[1].astype(F32), weight)
     block = column(hour_block[...], hours)
     blocks = block_price.shape[1]
     price = jnp.where(block == iota((hours, blocks), 1), block_price[...], 0.0)
@@ -92,7 +110,20 @@
         out[d] = pull[:, d * rows : (d + 1) * rows].astype(BF16)
 
 
-def first_body(arrived, ptdf, line_dual, limit, bus, parts, dual_out, unit_flow_out):
+def first_body(
+    here, arrived, ptdf, line_dual, bus, rating, index, leakage, hour_block, block_price, initial,
+    parts, dual_out, unit_flow_out, limit, growth, hour_price, chain, held, lefts, sems
+):
+    chunk = held.shape[0] // CHUNKS
+    spans = [pl.ds(k * chunk, chunk) for k in range(CHUNKS)]
+    copies = [
+        pltpu.make_async_copy(ptdf.at[at], held.at[at], sems.at[k]) for k, at in enumerate(spans)
+    ]
+    for copy in copies:
+        copy.start()
+    write_tables(
+        here, rating, index, leakage, hour_block, block_price, initial, limit, growth, hour_price, chain
+    )
     count, hours, width = arrived.shape
     rows = parts.shape[2]
     units = width - rows
@@ -109,20 +140,20 @@
         spread += lax.dot_general(
             jnp.concatenate(owned, axis=0), hot, NT, preferred_element_type=F32
         )
-    lefts = []
     for d in range(count):
         part = spread[d * hours : (d + 1) * hours]
         high = part.astype(BF16)
-        low = (part - high.astype(F32)).astype(BF16)
-        lefts.append(jnp.concatenate([arrived[d, :, :rows], high, low], axis=0))
-    products = lax.dot_general(
-        jnp.concatenate(lefts, axis=1), ptdf[...], NT, preferred_element_type=F32
-    )
-    unit_flow = products[hours : 2 * hours] + products[2 * hours :]
-    unit_flow_out[...] = unit_flow
-    dual = clipped(products[:hours] + unit_flow, line_dual[...], limit[...])
-    dual_out[...] = dual
-    pull_parts(dual, ptdf, parts)
+        at = slice(d * rows, (d + 1) * rows)
+        lefts[:hours, at] = arrived[d, :, :rows]
+        lefts[hours : 2 * hours, at] = high
+        lefts[2 * hours :, at] = (part - high.astype(F32)).astype(BF16)
+    for copy, at in zip(copies, spans):
+        copy.wait()
+        products = lax.dot_general(lefts[...], held[at], NT, preferred_element_type=F32)
+        unit_flow = products[hours : 2 * hours] + products[2 * hours :]
+        unit_flow_out[:, at] = unit_flow
+        dual_out[:, at] = clipped(products[:hours] + unit_flow, line_dual[:, at], limit[:, at])
+    pull_parts(dual_out[...], held, parts)
 
 
 def second_body(arrived, ptdf, line_dual, limit, unit_flow, parts, dual_out, mean_out):
@@ -207,14 +238,11 @@
     send[...] = jnp.broadcast_to(both[None], send.shape)
 
 
-def charge_body(here, arrived, pair, growth, initial, running, charge):
-    hours = growth.shape[0]
-    keep = growth[hours - 1 :]
-    twice = keep * keep
-    entering = initial[...]
-    for k in range(arrived.shape[0]):
-        entering = jnp.where(k < here[0], twice * entering + arrived[k, :1], entering)
-    entering = jnp.where(here[1] > 0, keep * entering + pair[0, :1], entering)
+def charge_body(arrived, pair, growth, chain, running, charge):
+    count = arrived.shape[0]
+    entering = chain[count : count + 1] + chain[count + 1 : count + 2] * pair[0, :1]
+    for k in range(count):
+        entering += chain[k : k + 1] * arrived[k, :1]
     charge[...] = growth[...] * entering + running[...]
 
 
@@ -249,22 +277,59 @@
     dual = line_dual.T
     cap, wear, initial = gen_cap[None], wear[None], initial_charge[None]
     price = balance_dual[None]
-    (packed,) = call(pack_body, "pack", shape((net, hours, rows + units), BF16))(gen, demand, held)
+    here = jnp.stack([lax.axis_index("tm_0"), lax.axis_index("tm_1")])
+    here, gen = lax.optimization_barrier((here, gen))
+    packed = pl.pallas_call(
+        pack_body,
+        name="pack",
+        in_specs=[pl.BlockSpec(memory_space=pltpu.HBM)] * 3,
+        out_shape=jax.ShapeDtypeStruct((net, hours, rows + units), BF16),
+        scratch_shapes=[
+            pltpu.VMEM((hours, rows), F32),
+            pltpu.VMEM((hours, rows), F32),
+            pltpu.VMEM((hours, units), F32),
+            pltpu.SemaphoreType.DMA((3,)),
+        ],
+        compiler_params=pltpu.CompilerParams(vmem_limit_bytes=VMEM_LIMIT),
+    )(*(pltpu.with_memory_space_constraint(a, pltpu.HBM) for a in (gen, demand, held)))
     arrived = everywhere(packed, "net")
-    limit, growth, hour_price = call(
-        tables_body,
-        "tables",
-        shape((1, lines), F32),
-        shape((hours, units), F32),
-        shape((hours, units), F32),
-    )(rating.reshape(-1, 128), line_index[None], leakage[None], hour_block[None], block_price[None])
-    parts, dual, unit_flow = call(
+    parts, dual, unit_flow, limit, growth, hour_price, chain, kept = pl.pallas_call(
         first_body,
-        "first",
-        shape((net, hours, rows), BF16),
-        shape((hours, lines), F32),
-        shape((hours, lines), F32),
-    )(arrived, ptdf, dual, limit, storage_bus[None])
+        name="first",
+        in_specs=[
+            pl.BlockSpec(memory_space=pltpu.SMEM),
+            pl.BlockSpec(),
+            pl.BlockSpec(memory_space=pltpu.HBM),
+        ]
+        + [pl.BlockSpec()] * 8,
+        out_shape=(
+            jax.ShapeDtypeStruct((net, hours, rows), BF16),
+            jax.ShapeDtypeStruct((hours, lines), F32),
+            jax.ShapeDtypeStruct((hours, lines), F32),
+            jax.ShapeDtypeStruct((1, lines), F32),
+            jax.ShapeDtypeStruct((hours, units), F32),
+            jax.ShapeDtypeStruct((hours, units), F32),
+            jax.ShapeDtypeStruct((chips + 8, units), F32),
+            jax.ShapeDtypeStruct(ptdf.shape, BF16),
+        ),
+        scratch_shapes=[
+            pltpu.VMEM((3 * hours, net * rows), BF16),
+            pltpu.SemaphoreType.DMA((CHUNKS,)),
+        ],
+        compiler_params=pltpu.CompilerParams(vmem_limit_bytes=VMEM_LIMIT),
+    )(
+        here,
+        arrived,
+        pltpu.with_memory_space_constraint(ptdf, pltpu.HBM),
+        dual,
+        storage_bus[None],
+        rating.reshape(-1, 128),
+        line_index[None],
+        leakage[None],
+        hour_block[None],
+        block_price[None],
+        initial,
+    )
     arrived = everywhere(parts, "net")
     send, trial = call(
         trial_body, "trial", shape((net, hours + 8, rows), F32), shape((hours, rows), F32)
@@ -276,7 +341,7 @@
         shape((net, hours, rows), BF16),
         shape((hours, lines), F32),
         shape((hours, 128), F32),
-    )(arrived, ptdf, dual, limit, unit_flow)
+    )(arrived, kept, dual, limit, unit_flow)
     arrived = everywhere(parts, "net")
     send, trial = call(
         last_trial_body, "last_trial", shape((net, 8, 128), F32), shape((hours, rows), F32)
@@ -294,15 +359,9 @@
     pair = lax.all_gather(last, "tm_1")
     (send,) = call(chip_body, "chip", shape((chips, 8, units), F32))(pair, growth)
     arrived = everywhere(send, "tm_0")
-    here = jnp.stack([lax.axis_index("tm_0"), lax.axis_index("tm_1")])
-    smem = pl.BlockSpec(memory_space=pltpu.SMEM)
-    vmem = pl.BlockSpec(memory_space=pltpu.VMEM)
-    charge = pl.pallas_call(
-        charge_body,
-        name="charge",
-        in_specs=[smem] + [vmem] * 5,
-        out_shape=jax.ShapeDtypeStruct((hours, units), F32),
-    )(here, arrived, pair, growth, initial, running)
+    (charge,) = call(charge_body, "charge", shape((hours, units), F32))(
+        arrived, pair, growth, chain, running
+    )
     return (gen.T, storage_next.T, charge.T, dual.T, price[0])
 
 

time: 137 us -> 133 us (0.971)
  blocking collectives: 59.8 us -> 109 us
  starting transfers between devices: 25.9 us -> 0 us
  waiting for transfers between devices: 22.3 us -> 0 us
  Pallas kernels: 22.9 us -> 17.4 us
  local copies, waits for them, and re-layouts: 3.74 us -> 5.71 us
    all_to_all x4 -> x6, blocking collectives: 49.8 us -> 99 us  [everywhere(): return lax.all_to_all(blocks, axis, split_axis=0, concat_axis=0, tiled=True)]
    all_to_all x2 -> x0, starting transfers between devices: 25.9 us -> none  [everywhere(): return lax.all_to_all(blocks, axis, split_axis=0, concat_axis=0, tiled=True)]
    all_to_all x2 -> x0, waiting for transfers between devices: 22.3 us -> none  [everywhere(): return lax.all_to_all(blocks, axis, split_axis=0, concat_axis=0, tiled=True)]
    pallas_call x1, Pallas kernels: 7.58 us -> 4.75 us  [per_device(): call(second_body, 'second', shape((net, hours, rows), BF16), shape((hours...]
    pallas_call x4 -> x3, Pallas kernels: 13.4 us -> 11.4 us  [the longest x1 9.76 us: per_device(): pl.pallas_call(first_body, name='first', in_specs=[pl.BlockSpec(memory_sp...]
    unnamed x42 -> x30, local copies, waits for them, and re-layouts: 3.74 us -> 5.71 us
  transfers between devices with their start and end apart: 2 -> 0, of which waited for: 2 -> 0; matrix products, arithmetic and copies ran while one was open for 0% -> 0% of each run, Pallas kernels for 0% -> 0%
where the time goes in v2:
time: 133 us
  blocking collectives  109 us (82%)
  Pallas kernels  17.4 us (13%)
  local copies, waits for them, and re-layouts  5.71 us (4%)
    all_to_all x6, blocking collectives, everywhere(): return lax.all_to_all(blocks, axis, split_axis=0, concat_axis=0, tiled=True)  99 us
    pallas_call x1, Pallas kernels, per_device(): pl.pallas_call(first_body, name='first', in_specs=[pl.BlockSpec(memory_sp...  9.76 us
    all_gather x1, blocking collectives, per_device(): pair = lax.all_gather(last, 'tm_1')  9.73 us
    unnamed x30, local copies, waits for them, and re-layouts  5.71 us
    pallas_call x1, Pallas kernels, per_device(): call(second_body, 'second', shape((net, hours, rows), BF16), shape((hours...  4.75 us

profile of v2, /device:TPU:1, one launch (start us, length us, event | category | flops | bytes accessed | tf_op | source)
XLA Modules:
  0.0 132.7 jit_solution(14454613879254041824)
XLA Ops:
  0.6 0.0 copy-start.4
  0.6 0.0 copy-start.1
  0.7 0.0 copy-start
  0.7 0.0 copy-start.7
  0.7 0.0 copy-start.9
  0.7 0.0 copy-start.3
  0.7 0.1 pad_add_fusion.here
  0.8 1.0 pack.1
  1.8 19.6 %all_to_all.30.arrived = bf16[16,64,384]{2,1,0:T(8,128)(2,1)S(1)} all-to-all(bf16[16,64,384]{2,1,0:T(8,128)(2,1)S(1)} %pack.1), channel_id=1, replica_groups=mesh['tm_0'=16,'tm_1'=2,'net'=16] {'net'}, dimensions={0} | all-to-all | bytes 1572864 | tf_op jit(solution)/shard_map/all_to_all | solution.py:250
  21.4 0.0 copy-start.2
  21.4 0.9 copy-done.2
  22.3 0.0 copy-start.5
  22.3 0.7 copy-done.5
  23.1 0.0 copy-start.6
  23.1 0.7 copy-done.6
  23.8 0.0 copy-start.8
  23.8 0.7 copy-done.8
  24.4 0.0 copy-start.10
  24.5 0.7 copy-done.10
  25.1 0.0 copy-start.11
  25.1 0.7 copy-done.11
  25.8 0.0 copy-start.12
  25.8 0.7 copy-done.12
  26.4 0.0 copy-start.13
  26.4 0.7 copy-done.13
  27.1 9.8 %first.1 = (bf16[16,64,256]{2,1,0:T(8,128)(2,1)S(1)}, f32[64,1024]{1,0:T(8,128)S(1)}, f32[64,1024]{1,0:T(8,128)S(1)}, f32[1,1024]{1,0:T(1,128)S(1)}, f32[64,128]...) custom-call(s32[2]{0:T(128)S(1)} %pad_add_fusion.here, ...), custom_call_target="tpu_custom_call" | custom-call | tf_op jit(solution)/shard_map/first/pallas_call | solution.py:296
  36.8 0.0 copy-start.14
  36.9 12.0 %all_to_all.31.arrived = bf16[16,64,256]{2,1,0:T(8,128)(2,1)S(1)} all-to-all(bf16[16,64,256]{2,1,0:T(8,128)(2,1)S(1)} %get-tuple-element.29), channel_id=1, replica_groups=mesh['tm_0'=16,'tm_1'=2,'net'=16] {'net'}, dimensions={0} | all-to-all | bytes 1048576 | tf_op jit(solution)/shard_map/all_to_all | solution.py:250
  48.9 0.0 copy-done.4
  48.9 0.0 copy-done.1
  48.9 0.0 copy-done
  48.9 0.0 copy-done.7
  48.9 0.0 copy-done.9
  48.9 0.0 copy-done.3
  48.9 0.2 trial.1
  49.1 17.0 %all_to_all.32.arrived = f32[16,72,256]{2,1,0:T(8,128)S(1)} all-to-all(f32[16,72,256]{2,1,0:T(8,128)S(1)} %get-tuple-element.30), channel_id=1, replica_groups=mesh['tm_0'=16,'tm_1'=2,'net'=16] {'net'}, dimensions={0} | all-to-all | bytes 2359296 | tf_op jit(solution)/shard_map/all_to_all | solution.py:250
  66.1 4.7 %second.1 = (bf16[16,64,256]{2,1,0:T(8,128)(2,1)S(1)}, f32[64,1024]{1,0:T(8,128)}, f32[64,128]{1,0:T(8,128)S(1)}) custom-call(f32[16,72,256]{2,1,0:T(8,128)S(1)} %all_to_all.32.arrived, bf16[1024,4096]{1,0:T(8,128)(2,1)S(1)} %get-tuple-element.31.ptdf, f32[64,1024]{1,0:T(8,128)S(1)} %get-tuple-element.32.line_dual, f32[1,1024]{1,0:T(1,128)S(1)} %get-tuple-element.33.limit, ...), custom_call_target="tpu_custom_call" | custom-call | tf_op jit(solution)/shard_map/second/pallas_call | solution.py:338
  70.9 11.6 %all_to_all.33.arrived = bf16[16,64,256]{2,1,0:T(8,128)(2,1)S(1)} all-to-all(bf16[16,64,256]{2,1,0:T(8,128)(2,1)S(1)} %get-tuple-element.35), channel_id=1, replica_groups=mesh['tm_0'=16,'tm_1'=2,'net'=16] {'net'}, dimensions={0} | all-to-all | bytes 1048576 | tf_op jit(solution)/shard_map/all_to_all | solution.py:250
  82.5 0.3 last_trial.1
  82.8 9.2 %all_to_all.34.arrived = f32[16,8,128]{2,1,0:T(8,128)S(1)} all-to-all(f32[16,8,128]{2,1,0:T(8,128)S(1)} %get-tuple-element.38), channel_id=1, replica_groups=mesh['tm_0'=16,'tm_1'=2,'net'=16] {'net'}, dimensions={0} | all-to-all | bytes 131072 | tf_op jit(solution)/shard_map/all_to_all | solution.py:250
  92.0 0.0 copy-done.14
  92.0 0.8 finish.1
  92.8 9.7 %all-gather = f32[16,128]{1,0:T(8,128)S(1)} all-gather(f32[8,128]{1,0:T(8,128)S(1)} %get-tuple-element.44), channel_id=2, replica_groups=mesh['tm_0'=16,'tm_1'=2,'net'=16] {'tm_1'}, dimensions={0}, use_global_device_ids=true | all-gather | bytes 12288 | tf_op jit(solution)/shard_map/all_gather | solution.py:359
  102.5 29.5 %all_to_all.35.arrived = f32[16,8,128]{2,1,0:T(8,128)S(1)} all-to-all(f32[16,8,128]{2,1,0:T(8,128)S(1)} %chip.1), channel_id=1, replica_groups=mesh['tm_0'=16,'tm_1'=2,'net'=16] {'tm_0'}, dimensions={0} | all-to-all | bytes 131072 | tf_op jit(solution)/shard_map/all_to_all | solution.py:250
  132.1 0.6 charge.1
  (1 shorter events, 0.0 us)
Async XLA Ops:
  0.6 48.2 %copy-start.4 = (f32[256,64]{0,1:T(8,128)S(1)}, f32[256,64]{0,1:T(8,128)}, u32[]{:S(2)}) copy-start(f32[256,64]{0,1:T(8,128)} %param.18) | copy-start | bytes 196612
  0.6 48.2 %copy-start.1 = (f32[128,64]{0,1:T(8,128)S(1)}, f32[128,64]{0,1:T(8,128)}, u32[]{:S(2)}) copy-start(f32[128,64]{0,1:T(8,128)} %param.21) | copy-start | bytes 98308
  0.7 48.2 %copy-start = (f32[256,64]{0,1:T(8,128)S(1)}, f32[256,64]{0,1:T(8,128)}, u32[]{:S(2)}) copy-start(f32[256,64]{0,1:T(8,128)} %param.17) | copy-start | bytes 196612
  0.7 48.2 %copy-start.7 = (f32[64]{0:T(128)S(1)}, f32[64]{0:T(128)}, u32[]{:S(2)}) copy-start(f32[64]{0:T(128)} %param.29) | copy-start | bytes 772
  0.7 48.2 %copy-start.9 = (f32[256]{0:T(256)S(1)}, f32[256]{0:T(256)}, u32[]{:S(2)}) copy-start(f32[256]{0:T(256)} %param.20) | copy-start | bytes 3076
  0.7 48.2 %copy-start.3 = (f32[256,64]{0,1:T(8,128)S(1)}, f32[256,64]{0,1:T(8,128)}, u32[]{:S(2)}) copy-start(f32[256,64]{0,1:T(8,128)} %param.19) | copy-start | bytes 196612
  21.4 1.0 copy-start.2
  22.3 0.7 copy-start.5
  23.1 0.7 copy-start.6
  23.8 0.7 copy-start.8
  24.4 0.7 copy-start.10
  25.1 0.7 copy-start.11
  25.8 0.7 copy-start.12
  26.4 0.7 copy-start.13
  36.8 55.1 %copy-start.14 = (f32[128]{0:T(128)S(1)}, f32[128]{0:T(128)}, u32[]{:S(2)}) copy-start(f32[128]{0:T(128)} %param.22) | copy-start | bytes 1540

commit v3 on v2

--- a/solution.py
+++ b/solution.py
@@ -111,9 +111,21 @@
 
 
 def first_body(
-    here, arrived, ptdf, line_dual, bus, rating, index, leakage, hour_block, block_price, initial,
-    parts, dual_out, unit_flow_out, limit, growth, hour_price, chain, held, lefts, sems
+    chip, core, arrived, ptdf,
+    bus_in, dual_in, rating_in, index_in, leakage_in, block_in, prices_in, initial_in,
+    parts, dual_out, unit_flow_out, row_sum, limit, growth, hour_price, chain, held,
+    bus, line_dual, rating, index, leakage, hour_block, block_price, initial,
+    lefts, owned, hot, small_sems, sems
 ):
+    here = chip[0], core[0]
+    sources = (bus_in, dual_in, rating_in, index_in, leakage_in, block_in, prices_in, initial_in)
+    targets = (bus, line_dual, rating, index, leakage, hour_block, block_price, initial)
+    small = [
+        pltpu.make_async_copy(a, b, small_sems.at[k])
+        for k, (a, b) in enumerate(zip(sources, targets))
+    ]
+    for copy in small:
+        copy.start()
     chunk = held.shape[0] // CHUNKS
     spans = [pl.ds(k * chunk, chunk) for k in range(CHUNKS)]
     copies = [
@@ -121,59 +133,74 @@
     ]
     for copy in copies:
         copy.start()
-    write_tables(
-        here, rating, index, leakage, hour_block, block_price, initial, limit, growth, hour_price, chain
-    )
     count, hours, width = arrived.shape
     rows = parts.shape[2]
     units = width - rows
-    spread = jnp.zeros((count * hours, rows), F32)
-    for k in range(0, count, 2):
-        at = bus[:, k * units : (k + 2) * units]
-        owner, place = at // rows, at % rows
-        storage = jnp.concatenate([arrived[k, :, rows:], arrived[k + 1, :, rows:]], axis=1)
-        hot = (iota((rows, 2 * units), 0) == place).astype(F32).astype(BF16)
-        owned = [
-            storage * jnp.broadcast_to((owner == d).astype(F32), storage.shape).astype(BF16)
-            for d in range(count)
-        ]
-        spread += lax.dot_general(
-            jnp.concatenate(owned, axis=0), hot, NT, preferred_element_type=F32
-        )
+    for d in range(count):
+        at = slice(d * rows, (d + 1) * rows)
+        lefts[:hours, at] = arrived[d, :, :rows]
+        lefts[3 * hours :, at] = (iota((count, rows), 0) == d).astype(F32).astype(BF16)
+    for copy in small:
+        copy.wait()
+    write_tables(
+        here, rating, index, leakage, hour_block, block_price, initial, limit, growth, hour_price, chain
+    )
+    owner, place = bus[...] // rows, bus[...] % rows
+    bus_row = iota((rows, units), 0)
+    for k in range(count):
+        at = slice(k * units, (k + 1) * units)
+        hot[:, at] = (bus_row == place[:, at]).astype(F32).astype(BF16)
+        for d in range(count):
+            mine = jnp.broadcast_to((owner[:, at] == d).astype(F32), (16, units)).astype(BF16)
+            for h in range(0, hours, 16):
+                owned[d * hours + h : d * hours + h + 16, at] = arrived[k, h : h + 16, rows:] * mine
+    spread = lax.dot_general(owned[...], hot[...], NT, preferred_element_type=F32)
     for d in range(count):
         part = spread[d * hours : (d + 1) * hours]
         high = part.astype(BF16)
         at = slice(d * rows, (d + 1) * rows)
-        lefts[:hours, at] = arrived[d, :, :rows]
         lefts[hours : 2 * hours, at] = high
-        lefts[2 * hours :, at] = (part - high.astype(F32)).astype(BF16)
+        lefts[2 * hours : 3 * hours, at] = (part - high.astype(F32)).astype(BF16)
     for copy, at in zip(copies, spans):
         copy.wait()
         products = lax.dot_general(lefts[...], held[at], NT, preferred_element_type=F32)
-        unit_flow = products[hours : 2 * hours] + products[2 * hours :]
+        unit_flow = products[hours : 2 * hours] + products[2 * hours : 3 * hours]
+        row_sum[:, at] = products[3 * hours :]
         unit_flow_out[:, at] = unit_flow
         dual_out[:, at] = clipped(products[:hours] + unit_flow, line_dual[:, at], limit[:, at])
     pull_parts(dual_out[...], held, parts)
 
 
-def second_body(arrived, ptdf, line_dual, limit, unit_flow, parts, dual_out, mean_out):
-    count, rows = parts.shape[0], parts.shape[2]
-    hours = parts.shape[1]
-    total = arrived[0, :hours]
-    extra = arrived[0, hours : hours + 1]
-    for d in range(1, count):
-        total += arrived[d, :hours]
-        extra += arrived[d, hours : hours + 1]
-    mismatch = jnp.sum(total, axis=1, keepdims=True) + column(extra, hours)
-    mean = mismatch / (count * rows)
-    mean_out[...] = jnp.broadcast_to(mean, mean_out.shape)
-    injection = [(arrived[d, :hours] - mean).astype(BF16) for d in range(count)]
-    flows = lax.dot_general(
-        jnp.concatenate(injection, axis=1), ptdf[...], NT, preferred_element_type=F32
+def second_body(arrived, ptdf, line_dual, limit, unit_flow, row_sum, parts, dual_out, mean_out):
+    count, hours, rows = parts.shape
+    notes = jnp.concatenate([arrived[d, hours : hours + 8] for d in range(count)], axis=0)
+    notes = notes.astype(F32)
+    notes = notes[:, :hours] + notes[:, hours : 2 * hours] + notes[:, 2 * hours : 3 * hours]
+    means = jnp.concatenate([notes[8 * d : 8 * d + 1] for d in range(count)], axis=0)
+    units = jnp.concatenate([notes[8 * d + 1 : 8 * d + 2] for d in range(count)], axis=0)
+    mean = jnp.sum(means * rows + units, axis=0, keepdims=True) / (count * rows)
+    mean_out[...] = jnp.broadcast_to(column(mean, hours), mean_out.shape)
+    balance = jnp.concatenate([arrived[d, :hours] for d in range(count)], axis=1)
+    flows = lax.dot_general(balance, ptdf[...], NT, preferred_element_type=F32)
+    flows += lax.dot_general(
+        means - mean,
+        row_sum[...],
+        (((0,), (0,)), ((), ())),
+        precision=lax.Precision.HIGHEST,
+        preferred_element_type=F32,
     )
     dual = clipped(flows + unit_flow[...], line_dual[...], limit[...])
     dual_out[...] = dual
     pull_parts(dual, ptdf, parts)
+
+
+def note(col, width):
+    n = col.shape[0]
+    high, middle, low = (part.astype(F32) for part in three_parts(col))
+    lane = iota((n, width), 1)
+    value = jnp.where(lane < n, high, jnp.where(lane < 2 * n, middle, low))
+    mine = (lane % n == iota((n, width), 0)) & (lane < 3 * n)
+    return jnp.sum(jnp.where(mine, value, 0.0), axis=0, keepdims=True)
 
 
 def total_of(arrived):
@@ -190,10 +217,15 @@
     trial = jnp.clip(gen[...] - STEP * (cost[...] - now + pull), 0.0, cap[...])
     trial_out[...] = trial
     balance = trial - demand[...]
-    unit_sum = row_of(jnp.sum(storage[...], axis=1, keepdims=True), send.shape[2])
-    below = jnp.broadcast_to(unit_sum, (send.shape[1] - hours, send.shape[2]))
+    width = balance.shape[1]
+    mean = jnp.sum(balance, axis=1, keepdims=True) / width
+    unit_sum = jnp.sum(storage[...], axis=1, keepdims=True)
+    row = iota((8, width), 0)
+    below = jnp.where(row == 0, note(mean, width), jnp.where(row == 1, note(unit_sum, width), 0.0))
+    below = below.astype(BF16)
+    around = (balance - mean).astype(BF16)
     for d in range(send.shape[0]):
-        send[d, :hours] = balance
+        send[d, :hours] = around
         send[d, hours:] = below
 
 
@@ -244,6 +276,10 @@
     for k in range(count):
         entering += chain[k : k + 1] * arrived[k, :1]
     charge[...] = growth[...] * entering + running[...]
+
+
+def in_hbm(array):
+    return pltpu.with_memory_space_constraint(array, pltpu.HBM)
 
 
 def everywhere(blocks, axis):
@@ -277,8 +313,9 @@
     dual = line_dual.T
     cap, wear, initial = gen_cap[None], wear[None], initial_charge[None]
     price = balance_dual[None]
-    here = jnp.stack([lax.axis_index("tm_0"), lax.axis_index("tm_1")])
-    here, gen = lax.optimization_barrier((here, gen))
+    chip, core, gen = lax.optimization_barrier(
+        (lax.axis_index("tm_0").reshape(1), lax.axis_index("tm_1").reshape(1), gen)
+    )
     packed = pl.pallas_call(
         pack_body,
         name="pack",
@@ -291,21 +328,28 @@
             pltpu.SemaphoreType.DMA((3,)),
         ],
         compiler_params=pltpu.CompilerParams(vmem_limit_bytes=VMEM_LIMIT),
-    )(*(pltpu.with_memory_space_constraint(a, pltpu.HBM) for a in (gen, demand, held)))
+    )(*(in_hbm(a) for a in (gen, demand, held)))
     arrived = everywhere(packed, "net")
-    parts, dual, unit_flow, limit, growth, hour_price, chain, kept = pl.pallas_call(
+    sources = (
+        storage_bus[None],
+        dual,
+        rating.reshape(-1, 128),
+        line_index[None],
+        leakage[None],
+        hour_block[None],
+        block_price[None],
+        initial,
+    )
+    smem, hbm = (pl.BlockSpec(memory_space=m) for m in (pltpu.SMEM, pltpu.HBM))
+    parts, dual, unit_flow, row_sum, limit, growth, hour_price, chain, kept = pl.pallas_call(
         first_body,
         name="first",
-        in_specs=[
-            pl.BlockSpec(memory_space=pltpu.SMEM),
-            pl.BlockSpec(),
-            pl.BlockSpec(memory_space=pltpu.HBM),
-        ]
-        + [pl.BlockSpec()] * 8,
+        in_specs=[smem, smem, pl.BlockSpec(), hbm] + [hbm] * len(sources),
         out_shape=(
             jax.ShapeDtypeStruct((net, hours, rows), BF16),
             jax.ShapeDtypeStruct((hours, lines), F32),
             jax.ShapeDtypeStruct((hours, lines), F32),
+            jax.ShapeDtypeStruct((net, lines), F32),
             jax.ShapeDtypeStruct((1, lines), F32),
             jax.ShapeDtypeStruct((hours, units), F32),
             jax.ShapeDtypeStruct((hours, units), F32),
@@ -313,26 +357,18 @@
             jax.ShapeDtypeStruct(ptdf.shape, BF16),
         ),
         scratch_shapes=[
-            pltpu.VMEM((3 * hours, net * rows), BF16),
+            *(pltpu.VMEM(a.shape, a.dtype) for a in sources),
+            pltpu.VMEM((3 * hours + net, net * rows), BF16),
+            pltpu.VMEM((net * hours, net * units), BF16),
+            pltpu.VMEM((rows, net * units), BF16),
+            pltpu.SemaphoreType.DMA((len(sources),)),
             pltpu.SemaphoreType.DMA((CHUNKS,)),
         ],
         compiler_params=pltpu.CompilerParams(vmem_limit_bytes=VMEM_LIMIT),
-    )(
-        here,
-        arrived,
-        pltpu.with_memory_space_constraint(ptdf, pltpu.HBM),
-        dual,
-        storage_bus[None],
-        rating.reshape(-1, 128),
-        line_index[None],
-        leakage[None],
-        hour_block[None],
-        block_price[None],
-        initial,
-    )
+    )(chip, core, arrived, *(in_hbm(a) for a in (ptdf, *sources)))
     arrived = everywhere(parts, "net")
     send, trial = call(
-        trial_body, "trial", shape((net, hours + 8, rows), F32), shape((hours, rows), F32)
+        trial_body, "trial", shape((net, hours + 8, rows), BF16), shape((hours, rows), F32)
     )(arrived, gen, cost, demand, price, cap, held)
     arrived = everywhere(send, "net")
     parts, dual, mean = call(
@@ -341,7 +377,7 @@
         shape((net, hours, rows), BF16),
         shape((hours, lines), F32),
         shape((hours, 128), F32),
-    )(arrived, kept, dual, limit, unit_flow)
+    )(arrived, kept, dual, limit, unit_flow, row_sum)
     arrived = everywhere(parts, "net")
     send, trial = call(
         last_trial_body, "last_trial", shape((net, 8, 128), F32), shape((hours, rows), F32)

time: 133 us -> 123 us (0.925)
  blocking collectives: 109 us -> 102 us
  local copies, waits for them, and re-layouts: 5.71 us -> 0.03 us
  Pallas kernels: 17.4 us -> 20.1 us
    all_to_all x6, blocking collectives: 99 us -> 92.6 us  [everywhere(): return lax.all_to_all(blocks, axis, split_axis=0, concat_axis=0, tiled=True)]
    unnamed x30 -> x14, local copies, waits for them, and re-layouts: 5.71 us -> 0.03 us
    pallas_call x2, Pallas kernels: 9.93 us -> 12.2 us  [the longest x1 12 us: per_device(): pl.pallas_call(first_body, name='first', in_specs=[smem, smem, pl.BlockSp...]
where the time goes in v3:
time: 123 us
  blocking collectives  102 us (83%)
  Pallas kernels  20.1 us (16%)
    all_to_all x6, blocking collectives, everywhere(): return lax.all_to_all(blocks, axis, split_axis=0, concat_axis=0, tiled=True)  92.6 us
    pallas_call x1, Pallas kernels, per_device(): pl.pallas_call(first_body, name='first', in_specs=[smem, smem, pl.BlockSp...  12 us
    all_gather x1, blocking collectives, per_device(): pair = lax.all_gather(last, 'tm_1')  9.6 us
    pallas_call x1, Pallas kernels, per_device(): call(second_body, 'second', shape((net, hours, rows), BF16), shape((hours...  5.05 us

profile of v3, /device:TPU:1, one launch (start us, length us, event | category | flops | bytes accessed | tf_op | source)
XLA Modules:
  0.0 123.1 jit_solution(14749374706916108047)
XLA Ops:
  0.6 0.0 copy-start.3
  0.6 0.0 copy-start.1
  0.7 0.0 copy-start
  0.7 0.0 copy-start.4
  0.7 0.0 copy-start.5
  0.7 0.0 copy-start.2
  0.7 1.1 pack.1
  1.8 19.6 %all_to_all.30.arrived = bf16[16,64,384]{2,1,0:T(8,128)(2,1)S(1)} all-to-all(bf16[16,64,384]{2,1,0:T(8,128)(2,1)S(1)} %pack.1), channel_id=1, replica_groups=mesh['tm_0'=16,'tm_1'=2,'net'=16] {'net'}, dimensions={0} | all-to-all | bytes 1572864 | tf_op jit(solution)/shard_map/all_to_all | solution.py:286
  21.4 12.0 %first.1 = (bf16[16,64,256]{2,1,0:T(8,128)(2,1)S(1)}, f32[64,1024]{1,0:T(8,128)S(1)}, f32[64,1024]{1,0:T(8,128)S(1)}, f32[16,1024]{1,0:T(8,128)S(1)}, f32[1,1024...) custom-call(s32[1]{0:T(128)} %bitcast.chip, ...), custom_call_target="tpu_custom_call" | custom-call | tf_op jit(solution)/shard_map/first/pallas_call | solution.py:344
  33.4 0.0 copy-start.6
  33.4 12.0 %all_to_all.31.arrived = bf16[16,64,256]{2,1,0:T(8,128)(2,1)S(1)} all-to-all(bf16[16,64,256]{2,1,0:T(8,128)(2,1)S(1)} %get-tuple-element.32), channel_id=1, replica_groups=mesh['tm_0'=16,'tm_1'=2,'net'=16] {'net'}, dimensions={0} | all-to-all | bytes 1048576 | tf_op jit(solution)/shard_map/all_to_all | solution.py:286
  45.4 0.0 copy-done.3
  45.4 0.0 copy-done.1
  45.4 0.0 copy-done
  45.4 0.0 copy-done.4
  45.5 0.0 copy-done.5
  45.5 0.0 copy-done.2
  45.5 0.2 trial.1
  45.7 12.1 %all_to_all.32.arrived = bf16[16,72,256]{2,1,0:T(8,128)(2,1)S(1)} all-to-all(bf16[16,72,256]{2,1,0:T(8,128)(2,1)S(1)} %get-tuple-element.33), channel_id=1, replica_groups=mesh['tm_0'=16,'tm_1'=2,'net'=16] {'net'}, dimensions={0} | all-to-all | bytes 1179648 | tf_op jit(solution)/shard_map/all_to_all | solution.py:286
  57.8 5.1 %second.1 = (bf16[16,64,256]{2,1,0:T(8,128)(2,1)S(1)}, f32[64,1024]{1,0:T(8,128)}, f32[64,128]{1,0:T(8,128)S(1)}) custom-call(bf16[16,72,256]{2,1,0:T(8,128)(2,1)S(1)} %all_to_all.32.arrived, bf16[1024,4096]{1,0:T(8,128)(2,1)S(1)} %get-tuple-element.34.ptdf, f32[64,1024]{1,0:T(8,128)S(1)} %get-tuple-element.35.line_dual, ...), custom_call_target="tpu_custom_call" | custom-call | tf_op jit(solution)/shard_map/second/pallas_call | solution.py:374
  62.9 12.1 %all_to_all.33.arrived = bf16[16,64,256]{2,1,0:T(8,128)(2,1)S(1)} all-to-all(bf16[16,64,256]{2,1,0:T(8,128)(2,1)S(1)} %get-tuple-element.39), channel_id=1, replica_groups=mesh['tm_0'=16,'tm_1'=2,'net'=16] {'net'}, dimensions={0} | all-to-all | bytes 1048576 | tf_op jit(solution)/shard_map/all_to_all | solution.py:286
  74.9 0.3 last_trial.1
  75.2 9.2 %all_to_all.34.arrived = f32[16,8,128]{2,1,0:T(8,128)S(1)} all-to-all(f32[16,8,128]{2,1,0:T(8,128)S(1)} %get-tuple-element.42), channel_id=1, replica_groups=mesh['tm_0'=16,'tm_1'=2,'net'=16] {'net'}, dimensions={0} | all-to-all | bytes 131072 | tf_op jit(solution)/shard_map/all_to_all | solution.py:286
  84.4 0.0 copy-done.6
  84.4 0.8 finish.1
  85.2 9.6 %all-gather = f32[16,128]{1,0:T(8,128)S(1)} all-gather(f32[8,128]{1,0:T(8,128)S(1)} %get-tuple-element.48), channel_id=2, replica_groups=mesh['tm_0'=16,'tm_1'=2,'net'=16] {'tm_1'}, dimensions={0}, use_global_device_ids=true | all-gather | bytes 12288 | tf_op jit(solution)/shard_map/all_gather | solution.py:395
  94.8 27.6 %all_to_all.35.arrived = f32[16,8,128]{2,1,0:T(8,128)S(1)} all-to-all(f32[16,8,128]{2,1,0:T(8,128)S(1)} %chip.1), channel_id=1, replica_groups=mesh['tm_0'=16,'tm_1'=2,'net'=16] {'tm_0'}, dimensions={0} | all-to-all | bytes 131072 | tf_op jit(solution)/shard_map/all_to_all | solution.py:286
  122.4 0.6 charge.1
  (1 shorter events, 0.0 us)
Async XLA Ops:
  0.6 44.8 %copy-start.3 = (f32[256,64]{0,1:T(8,128)S(1)}, f32[256,64]{0,1:T(8,128)}, u32[]{:S(2)}) copy-start(f32[256,64]{0,1:T(8,128)} %param.18) | copy-start | bytes 196612
  0.6 44.8 %copy-start.1 = (f32[128,64]{0,1:T(8,128)S(1)}, f32[128,64]{0,1:T(8,128)}, u32[]{:S(2)}) copy-start(f32[128,64]{0,1:T(8,128)} %param.21) | copy-start | bytes 98308
  0.7 44.8 %copy-start = (f32[256,64]{0,1:T(8,128)S(1)}, f32[256,64]{0,1:T(8,128)}, u32[]{:S(2)}) copy-start(f32[256,64]{0,1:T(8,128)} %param.17) | copy-start | bytes 196612
  0.7 44.8 %copy-start.4 = (f32[64]{0:T(128)S(1)}, f32[64]{0:T(128)}, u32[]{:S(2)}) copy-start(f32[64]{0:T(128)} %param.29) | copy-start | bytes 772
  0.7 44.8 %copy-start.5 = (f32[256]{0:T(256)S(1)}, f32[256]{0:T(256)}, u32[]{:S(2)}) copy-start(f32[256]{0:T(256)} %param.20) | copy-start | bytes 3076
  0.7 44.8 %copy-start.2 = (f32[256,64]{0,1:T(8,128)S(1)}, f32[256,64]{0,1:T(8,128)}, u32[]{:S(2)}) copy-start(f32[256,64]{0,1:T(8,128)} %param.19) | copy-start | bytes 196612
  33.4 51.0 %copy-start.6 = (f32[128]{0:T(128)S(1)}, f32[128]{0:T(128)}, u32[]{:S(2)}) copy-start(f32[128]{0:T(128)} %param.22) | copy-start | bytes 1540

commit v4 on v3

--- a/solution.py
+++ b/solution.py
@@ -15,7 +15,6 @@
 
 F32 = jnp.float32
 VMEM_LIMIT = 16 << 20
-CHUNKS = 4
 BF16 = jnp.bfloat16
 NT = (((1,), (1,)), ((), ()))
 
@@ -56,13 +55,34 @@
     return high, middle, low
 
 
-def pack_body(gen_in, demand_in, storage_in, out, gen, demand, storage, sems):
-    pairs = ((gen_in, gen), (demand_in, demand), (storage_in, storage))
+def pack_body(
+    chip, core, gen_in, demand_in, storage_in, bus_in, dual_in, rating_in, index_in, leakage_in,
+    block_in, prices_in, initial_in,
+    out, limit, growth, hour_price, chain, bus, line_dual,
+    gen, demand, storage, rating, index, leakage, hour_block, block_price, initial, sems
+):
+    pairs = (
+        (gen_in, gen),
+        (demand_in, demand),
+        (storage_in, storage),
+        (rating_in, rating),
+        (index_in, index),
+        (leakage_in, leakage),
+        (block_in, hour_block),
+        (prices_in, block_price),
+        (initial_in, initial),
+        (bus_in, bus),
+        (dual_in, line_dual),
+    )
     copies = [pltpu.make_async_copy(a, b, sems.at[k]) for k, (a, b) in enumerate(pairs)]
     for copy in copies:
         copy.start()
     for copy in copies:
         copy.wait()
+    here = chip[0], core[0]
+    write_tables(
+        here, rating, index, leakage, hour_block, block_price, initial, limit, growth, hour_price, chain
+    )
     rows = gen.shape[1]
     injection = (gen[...] - demand[...]).astype(BF16)
     units = storage[...].astype(BF16)
@@ -111,28 +131,11 @@
 
 
 def first_body(
-    chip, core, arrived, ptdf,
-    bus_in, dual_in, rating_in, index_in, leakage_in, block_in, prices_in, initial_in,
-    parts, dual_out, unit_flow_out, row_sum, limit, growth, hour_price, chain, held,
-    bus, line_dual, rating, index, leakage, hour_block, block_price, initial,
-    lefts, owned, hot, small_sems, sems
+    arrived, ptdf, bus, line_dual, limit, parts, dual_out, unit_flow_out, row_sum, held,
+    lefts, owned, hot, sem
 ):
-    here = chip[0], core[0]
-    sources = (bus_in, dual_in, rating_in, index_in, leakage_in, block_in, prices_in, initial_in)
-    targets = (bus, line_dual, rating, index, leakage, hour_block, block_price, initial)
-    small = [
-        pltpu.make_async_copy(a, b, small_sems.at[k])
-        for k, (a, b) in enumerate(zip(sources, targets))
-    ]
-    for copy in small:
-        copy.start()
-    chunk = held.shape[0] // CHUNKS
-    spans = [pl.ds(k * chunk, chunk) for k in range(CHUNKS)]
-    copies = [
-        pltpu.make_async_copy(ptdf.at[at], held.at[at], sems.at[k]) for k, at in enumerate(spans)
-    ]
-    for copy in copies:
-        copy.start()
+    copy = pltpu.make_async_copy(ptdf, held, sem)
+    copy.start()
     count, hours, width = arrived.shape
     rows = parts.shape[2]
     units = width - rows
@@ -140,11 +143,6 @@
         at = slice(d * rows, (d + 1) * rows)
         lefts[:hours, at] = arrived[d, :, :rows]
         lefts[3 * hours :, at] = (iota((count, rows), 0) == d).astype(F32).astype(BF16)
-    for copy in small:
-        copy.wait()
-    write_tables(
-        here, rating, index, leakage, hour_block, block_price, initial, limit, growth, hour_price, chain
-    )
     owner, place = bus[...] // rows, bus[...] % rows
     bus_row = iota((rows, units), 0)
     for k in range(count):
@@ -161,14 +159,14 @@
         at = slice(d * rows, (d + 1) * rows)
         lefts[hours : 2 * hours, at] = high
         lefts[2 * hours : 3 * hours, at] = (part - high.astype(F32)).astype(BF16)
-    for copy, at in zip(copies, spans):
-        copy.wait()
-        products = lax.dot_general(lefts[...], held[at], NT, preferred_element_type=F32)
-        unit_flow = products[hours : 2 * hours] + products[2 * hours : 3 * hours]
-        row_sum[:, at] = products[3 * hours :]
-        unit_flow_out[:, at] = unit_flow
-        dual_out[:, at] = clipped(products[:hours] + unit_flow, line_dual[:, at], limit[:, at])
-    pull_parts(dual_out[...], held, parts)
+    copy.wait()
+    products = lax.dot_general(lefts[...], held[...], NT, preferred_element_type=F32)
+    unit_flow = products[hours : 2 * hours] + products[2 * hours : 3 * hours]
+    row_sum[...] = products[3 * hours :]
+    unit_flow_out[...] = unit_flow
+    dual = clipped(products[:hours] + unit_flow, line_dual[...], limit[...])
+    dual_out[...] = dual
+    pull_parts(dual, held, parts)
 
 
 def second_body(arrived, ptdf, line_dual, limit, unit_flow, row_sum, parts, dual_out, mean_out):
@@ -316,21 +314,10 @@
     chip, core, gen = lax.optimization_barrier(
         (lax.axis_index("tm_0").reshape(1), lax.axis_index("tm_1").reshape(1), gen)
     )
-    packed = pl.pallas_call(
-        pack_body,
-        name="pack",
-        in_specs=[pl.BlockSpec(memory_space=pltpu.HBM)] * 3,
-        out_shape=jax.ShapeDtypeStruct((net, hours, rows + units), BF16),
-        scratch_shapes=[
-            pltpu.VMEM((hours, rows), F32),
-            pltpu.VMEM((hours, rows), F32),
-            pltpu.VMEM((hours, units), F32),
-            pltpu.SemaphoreType.DMA((3,)),
-        ],
-        compiler_params=pltpu.CompilerParams(vmem_limit_bytes=VMEM_LIMIT),
-    )(*(in_hbm(a) for a in (gen, demand, held)))
-    arrived = everywhere(packed, "net")
     sources = (
+        gen,
+        demand,
+        held,
         storage_bus[None],
         dual,
         rating.reshape(-1, 128),
@@ -341,31 +328,45 @@
         initial,
     )
     smem, hbm = (pl.BlockSpec(memory_space=m) for m in (pltpu.SMEM, pltpu.HBM))
-    parts, dual, unit_flow, row_sum, limit, growth, hour_price, chain, kept = pl.pallas_call(
+    packed, limit, growth, hour_price, chain, bus, dual = pl.pallas_call(
+        pack_body,
+        name="pack",
+        in_specs=[smem, smem] + [hbm] * len(sources),
+        out_shape=(
+            jax.ShapeDtypeStruct((net, hours, rows + units), BF16),
+            jax.ShapeDtypeStruct((1, lines), F32),
+            jax.ShapeDtypeStruct((hours, units), F32),
+            jax.ShapeDtypeStruct((hours, units), F32),
+            jax.ShapeDtypeStruct((chips + 8, units), F32),
+            jax.ShapeDtypeStruct((1, net * units), jnp.int32),
+            jax.ShapeDtypeStruct((hours, lines), F32),
+        ),
+        scratch_shapes=[
+            *(pltpu.VMEM(a.shape, a.dtype) for a in sources[:3] + sources[5:]),
+            pltpu.SemaphoreType.DMA((len(sources),)),
+        ],
+        compiler_params=pltpu.CompilerParams(vmem_limit_bytes=VMEM_LIMIT),
+    )(chip, core, *(in_hbm(a) for a in sources))
+    arrived = everywhere(packed, "net")
+    parts, dual, unit_flow, row_sum, ptdf = pl.pallas_call(
         first_body,
         name="first",
-        in_specs=[smem, smem, pl.BlockSpec(), hbm] + [hbm] * len(sources),
+        in_specs=[pl.BlockSpec(), hbm] + [pl.BlockSpec()] * 3,
         out_shape=(
             jax.ShapeDtypeStruct((net, hours, rows), BF16),
             jax.ShapeDtypeStruct((hours, lines), F32),
             jax.ShapeDtypeStruct((hours, lines), F32),
             jax.ShapeDtypeStruct((net, lines), F32),
-            jax.ShapeDtypeStruct((1, lines), F32),
-            jax.ShapeDtypeStruct((hours, units), F32),
-            jax.ShapeDtypeStruct((hours, units), F32),
-            jax.ShapeDtypeStruct((chips + 8, units), F32),
             jax.ShapeDtypeStruct(ptdf.shape, BF16),
         ),
         scratch_shapes=[
-            *(pltpu.VMEM(a.shape, a.dtype) for a in sources),
             pltpu.VMEM((3 * hours + net, net * rows), BF16),
             pltpu.VMEM((net * hours, net * units), BF16),
             pltpu.VMEM((rows, net * units), BF16),
-            pltpu.SemaphoreType.DMA((len(sources),)),
-            pltpu.SemaphoreType.DMA((CHUNKS,)),
+            pltpu.SemaphoreType.DMA(()),
         ],
         compiler_params=pltpu.CompilerParams(vmem_limit_bytes=VMEM_LIMIT),
-    )(chip, core, arrived, *(in_hbm(a) for a in (ptdf, *sources)))
+    )(arrived, in_hbm(ptdf), bus, dual, limit)
     arrived = everywhere(parts, "net")
     send, trial = call(
         trial_body, "trial", shape((net, hours + 8, rows), BF16), shape((hours, rows), F32)
@@ -377,7 +378,7 @@
         shape((net, hours, rows), BF16),
         shape((hours, lines), F32),
         shape((hours, 128), F32),
-    )(arrived, kept, dual, limit, unit_flow, row_sum)
+    )(arrived, ptdf, dual, limit, unit_flow, row_sum)
     arrived = everywhere(parts, "net")
     send, trial = call(
         last_trial_body, "last_trial", shape((net, 8, 128), F32), shape((hours, rows), F32)

time: 123 us -> 120 us (0.976)
  Pallas kernels: 20.1 us -> 17 us
    pallas_call x2, Pallas kernels: 13.1 us -> 9.93 us  [the longest x1 8.25 us: per_device(): pl.pallas_call(first_body, name='first', in_specs=[pl.BlockSpec(), hbm] +...]
where the time goes in v4:
time: 120 us
  blocking collectives  102 us (85%)
  Pallas kernels  17 us (14%)
    all_to_all x6, blocking collectives, everywhere(): return lax.all_to_all(blocks, axis, split_axis=0, concat_axis=0, tiled=True)  92.6 us
    all_gather x1, blocking collectives, per_device(): pair = lax.all_gather(last, 'tm_1')  9.6 us
    pallas_call x1, Pallas kernels, per_device(): pl.pallas_call(first_body, name='first', in_specs=[pl.BlockSpec(), hbm] +...  8.25 us
    pallas_call x1, Pallas kernels, per_device(): call(second_body, 'second', shape((net, hours, rows), BF16), shape((hours...  5.06 us

profile of v4, /device:TPU:1, one launch (start us, length us, event | category | flops | bytes accessed | tf_op | source)
XLA Modules:
  0.0 119.9 jit_solution(9414176561939875475)
XLA Ops:
  0.6 0.0 copy-start.2
  0.6 0.0 copy-start.1
  0.7 0.0 copy-start
  0.7 0.0 copy-start.4
  0.7 0.0 copy-start.5
  0.7 0.0 copy-start.3
  0.7 1.7 %pack.1 = (bf16[16,64,384]{2,1,0:T(8,128)(2,1)S(1)}, f32[1,1024]{1,0:T(1,128)S(1)}, f32[64,128]{1,0:T(8,128)S(1)}, f32[64,128]{1,0:T(8,128)S(1)}, f32[24,128]{1,...) custom-call(s32[1]{0:T(128)} %bitcast.chip, s32[1]{0:T(128)} %bitcast.1.core, f32[64,256]{1,0:T(8,128)} %bitcast.30, ...), custom_call_target="tpu_custom_call" | custom-call | tf_op jit(solution)/shard_map/pack/pallas_call | solution.py:331
  2.4 19.6 %all_to_all.30.arrived = bf16[16,64,384]{2,1,0:T(8,128)(2,1)S(1)} all-to-all(bf16[16,64,384]{2,1,0:T(8,128)(2,1)S(1)} %get-tuple-element.35), channel_id=1, replica_groups=mesh['tm_0'=16,'tm_1'=2,'net'=16] {'net'}, dimensions={0} | all-to-all | bytes 1572864 | tf_op jit(solution)/shard_map/all_to_all | solution.py:284
  22.0 8.3 %first.1 = (bf16[16,64,256]{2,1,0:T(8,128)(2,1)S(1)}, f32[64,1024]{1,0:T(8,128)S(1)}, f32[64,1024]{1,0:T(8,128)S(1)}, f32[16,1024]{1,0:T(8,128)S(1)}, bf16[1024,4096]{1,0:T(8,128)(2,1)S(1)}) custom-call(bf16[16,64,384]{2,1,0:T(8,128)(2,1)S(1)} %all_to_all.30.arrived, bf16[1024,4096]{1,0:T(8,128)(2,1)} %ptdf.1, s32[1,2048]{1,0:T(1,128)S(1)} %get-tuple-element.36.bus, ...), custom_call_target="tpu_custom_call" | custom-call | tf_op jit(solution)/shard_map/first/pallas_call | solution.py:351
  30.3 0.0 copy-start.6
  30.3 12.0 %all_to_all.31.arrived = bf16[16,64,256]{2,1,0:T(8,128)(2,1)S(1)} all-to-all(bf16[16,64,256]{2,1,0:T(8,128)(2,1)S(1)} %get-tuple-element.39), channel_id=1, replica_groups=mesh['tm_0'=16,'tm_1'=2,'net'=16] {'net'}, dimensions={0} | all-to-all | bytes 1048576 | tf_op jit(solution)/shard_map/all_to_all | solution.py:284
  42.3 0.0 copy-done.2
  42.3 0.0 copy-done.1
  42.3 0.0 copy-done
  42.3 0.0 copy-done.4
  42.3 0.0 copy-done.5
  42.3 0.0 copy-done.3
  42.3 0.2 trial.1
  42.5 12.1 %all_to_all.32.arrived = bf16[16,72,256]{2,1,0:T(8,128)(2,1)S(1)} all-to-all(bf16[16,72,256]{2,1,0:T(8,128)(2,1)S(1)} %get-tuple-element.40), channel_id=1, replica_groups=mesh['tm_0'=16,'tm_1'=2,'net'=16] {'net'}, dimensions={0} | all-to-all | bytes 1179648 | tf_op jit(solution)/shard_map/all_to_all | solution.py:284
  54.6 5.1 %second.1 = (bf16[16,64,256]{2,1,0:T(8,128)(2,1)S(1)}, f32[64,1024]{1,0:T(8,128)}, f32[64,128]{1,0:T(8,128)S(1)}) custom-call(bf16[16,72,256]{2,1,0:T(8,128)(2,1)S(1)} %all_to_all.32.arrived, bf16[1024,4096]{1,0:T(8,128)(2,1)S(1)} %get-tuple-element.41.ptdf, f32[64,1024]{1,0:T(8,128)S(1)} %get-tuple-element.42.line_dual, ...), custom_call_target="tpu_custom_call" | custom-call | tf_op jit(solution)/shard_map/second/pallas_call | solution.py:375
  59.7 12.1 %all_to_all.33.arrived = bf16[16,64,256]{2,1,0:T(8,128)(2,1)S(1)} all-to-all(bf16[16,64,256]{2,1,0:T(8,128)(2,1)S(1)} %get-tuple-element.45), channel_id=1, replica_groups=mesh['tm_0'=16,'tm_1'=2,'net'=16] {'net'}, dimensions={0} | all-to-all | bytes 1048576 | tf_op jit(solution)/shard_map/all_to_all | solution.py:284
  71.8 0.3 last_trial.1
  72.0 9.2 %all_to_all.34.arrived = f32[16,8,128]{2,1,0:T(8,128)S(1)} all-to-all(f32[16,8,128]{2,1,0:T(8,128)S(1)} %get-tuple-element.48), channel_id=1, replica_groups=mesh['tm_0'=16,'tm_1'=2,'net'=16] {'net'}, dimensions={0} | all-to-all | bytes 131072 | tf_op jit(solution)/shard_map/all_to_all | solution.py:284
  81.2 0.0 copy-done.6
  81.2 0.8 finish.1
  82.1 9.6 %all-gather = f32[16,128]{1,0:T(8,128)S(1)} all-gather(f32[8,128]{1,0:T(8,128)S(1)} %get-tuple-element.54), channel_id=2, replica_groups=mesh['tm_0'=16,'tm_1'=2,'net'=16] {'tm_1'}, dimensions={0}, use_global_device_ids=true | all-gather | bytes 12288 | tf_op jit(solution)/shard_map/all_gather | solution.py:396
  91.7 27.6 %all_to_all.35.arrived = f32[16,8,128]{2,1,0:T(8,128)S(1)} all-to-all(f32[16,8,128]{2,1,0:T(8,128)S(1)} %chip.1), channel_id=1, replica_groups=mesh['tm_0'=16,'tm_1'=2,'net'=16] {'tm_0'}, dimensions={0} | all-to-all | bytes 131072 | tf_op jit(solution)/shard_map/all_to_all | solution.py:284
  119.3 0.6 charge.1
  (1 shorter events, 0.0 us)
Async XLA Ops:
  0.6 41.6 %copy-start.2 = (f32[256,64]{0,1:T(8,128)S(1)}, f32[256,64]{0,1:T(8,128)}, u32[]{:S(2)}) copy-start(f32[256,64]{0,1:T(8,128)} %param.18) | copy-start | bytes 196612
  0.6 41.6 %copy-start.1 = (f32[128,64]{0,1:T(8,128)S(1)}, f32[128,64]{0,1:T(8,128)}, u32[]{:S(2)}) copy-start(f32[128,64]{0,1:T(8,128)} %param.21) | copy-start | bytes 98308
  0.7 41.6 %copy-start = (f32[256,64]{0,1:T(8,128)S(1)}, f32[256,64]{0,1:T(8,128)}, u32[]{:S(2)}) copy-start(f32[256,64]{0,1:T(8,128)} %param.17) | copy-start | bytes 196612
  0.7 41.6 %copy-start.4 = (f32[64]{0:T(128)S(1)}, f32[64]{0:T(128)}, u32[]{:S(2)}) copy-start(f32[64]{0:T(128)} %param.29) | copy-start | bytes 772
  0.7 41.6 %copy-start.5 = (f32[256]{0:T(256)S(1)}, f32[256]{0:T(256)}, u32[]{:S(2)}) copy-start(f32[256]{0:T(256)} %param.20) | copy-start | bytes 3076
  0.7 41.6 %copy-start.3 = (f32[256,64]{0,1:T(8,128)S(1)}, f32[256,64]{0,1:T(8,128)}, u32[]{:S(2)}) copy-start(f32[256,64]{0,1:T(8,128)} %param.19) | copy-start | bytes 196612
  30.3 51.0 %copy-start.6 = (f32[128]{0:T(128)S(1)}, f32[128]{0:T(128)}, u32[]{:S(2)}) copy-start(f32[128]{0:T(128)} %param.22) | copy-start | bytes 1540

commit v5 on v4

--- a/solution.py
+++ b/solution.py
@@ -15,6 +15,7 @@
 
 F32 = jnp.float32
 VMEM_LIMIT = 16 << 20
+EARLY = 6
 BF16 = jnp.bfloat16
 NT = (((1,), (1,)), ((), ()))
 
@@ -57,8 +58,8 @@
 
 def pack_body(
     chip, core, gen_in, demand_in, storage_in, bus_in, dual_in, rating_in, index_in, leakage_in,
-    block_in, prices_in, initial_in,
-    out, limit, growth, hour_price, chain, bus, line_dual,
+    block_in, prices_in, initial_in, ptdf,
+    out, limit, growth, hour_price, chain, bus, line_dual, begun,
     gen, demand, storage, rating, index, leakage, hour_block, block_price, initial, sems
 ):
     pairs = (
@@ -77,18 +78,24 @@
     copies = [pltpu.make_async_copy(a, b, sems.at[k]) for k, (a, b) in enumerate(pairs)]
     for copy in copies:
         copy.start()
-    for copy in copies:
+    first_rows = pl.ds(0, begun.shape[0] * EARLY // 16)
+    early = pltpu.make_async_copy(ptdf.at[first_rows], begun.at[first_rows], sems.at[len(pairs)])
+    early.start()
+    for copy in copies[:3]:
         copy.wait()
-    here = chip[0], core[0]
-    write_tables(
-        here, rating, index, leakage, hour_block, block_price, initial, limit, growth, hour_price, chain
-    )
     rows = gen.shape[1]
     injection = (gen[...] - demand[...]).astype(BF16)
     units = storage[...].astype(BF16)
     for d in range(out.shape[0]):
         out[d, :, :rows] = injection
         out[d, :, rows:] = units
+    for copy in copies[3:]:
+        copy.wait()
+    here = chip[0], core[0]
+    write_tables(
+        here, rating, index, leakage, hour_block, block_price, initial, limit, growth, hour_price, chain
+    )
+    early.wait()
 
 
 def write_tables(
@@ -131,10 +138,12 @@
 
 
 def first_body(
-    arrived, ptdf, bus, line_dual, limit, parts, dual_out, unit_flow_out, row_sum, held,
+    arrived, ptdf, bus, line_dual, limit, begun, parts, dual_out, unit_flow_out, row_sum, held,
     lefts, owned, hot, sem
 ):
-    copy = pltpu.make_async_copy(ptdf, held, sem)
+    early = held.shape[0] * EARLY // 16
+    rest = pl.ds(early, held.shape[0] - early)
+    copy = pltpu.make_async_copy(ptdf.at[rest], held.at[rest], sem)
     copy.start()
     count, hours, width = arrived.shape
     rows = parts.shape[2]
@@ -268,12 +277,24 @@
     send[...] = jnp.broadcast_to(both[None], send.shape)
 
 
-def charge_body(arrived, pair, growth, chain, running, charge):
+def charge_body(
+    arrived, pair, growth, chain, running, gen, storage, dual, price,
+    charge_out, gen_out, storage_out, dual_out, price_out, charge, sems
+):
+    done = ((gen, gen_out), (storage, storage_out), (dual, dual_out), (price, price_out))
+    copies = [pltpu.make_async_copy(a, b, sems.at[k]) for k, (a, b) in enumerate(done)]
+    for copy in copies:
+        copy.start()
     count = arrived.shape[0]
     entering = chain[count : count + 1] + chain[count + 1 : count + 2] * pair[0, :1]
     for k in range(count):
         entering += chain[k : k + 1] * arrived[k, :1]
     charge[...] = growth[...] * entering + running[...]
+    last = pltpu.make_async_copy(charge, charge_out, sems.at[len(done)])
+    last.start()
+    for copy in copies:
+        copy.wait()
+    last.wait()
 
 
 def in_hbm(array):
@@ -328,10 +349,10 @@
         initial,
     )
     smem, hbm = (pl.BlockSpec(memory_space=m) for m in (pltpu.SMEM, pltpu.HBM))
-    packed, limit, growth, hour_price, chain, bus, dual = pl.pallas_call(
+    packed, limit, growth, hour_price, chain, bus, dual, begun = pl.pallas_call(
         pack_body,
         name="pack",
-        in_specs=[smem, smem] + [hbm] * len(sources),
+        in_specs=[smem, smem] + [hbm] * (len(sources) + 1),
         out_shape=(
             jax.ShapeDtypeStruct((net, hours, rows + units), BF16),
             jax.ShapeDtypeStruct((1, lines), F32),
@@ -340,18 +361,20 @@
             jax.ShapeDtypeStruct((chips + 8, units), F32),
             jax.ShapeDtypeStruct((1, net * units), jnp.int32),
             jax.ShapeDtypeStruct((hours, lines), F32),
+            jax.ShapeDtypeStruct(ptdf.shape, BF16),
         ),
         scratch_shapes=[
             *(pltpu.VMEM(a.shape, a.dtype) for a in sources[:3] + sources[5:]),
-            pltpu.SemaphoreType.DMA((len(sources),)),
+            pltpu.SemaphoreType.DMA((len(sources) + 1,)),
         ],
         compiler_params=pltpu.CompilerParams(vmem_limit_bytes=VMEM_LIMIT),
-    )(chip, core, *(in_hbm(a) for a in sources))
+    )(chip, core, *(in_hbm(a) for a in (*sources, ptdf)))
     arrived = everywhere(packed, "net")
     parts, dual, unit_flow, row_sum, ptdf = pl.pallas_call(
         first_body,
         name="first",
-        in_specs=[pl.BlockSpec(), hbm] + [pl.BlockSpec()] * 3,
+        in_specs=[pl.BlockSpec(), hbm] + [pl.BlockSpec()] * 4,
+        input_output_aliases={5: 4},
         out_shape=(
             jax.ShapeDtypeStruct((net, hours, rows), BF16),
             jax.ShapeDtypeStruct((hours, lines), F32),
@@ -366,7 +389,7 @@
             pltpu.SemaphoreType.DMA(()),
         ],
         compiler_params=pltpu.CompilerParams(vmem_limit_bytes=VMEM_LIMIT),
-    )(arrived, in_hbm(ptdf), bus, dual, limit)
+    )(arrived, in_hbm(ptdf), bus, dual, limit, begun)
     arrived = everywhere(parts, "net")
     send, trial = call(
         trial_body, "trial", shape((net, hours + 8, rows), BF16), shape((hours, rows), F32)
@@ -396,9 +419,16 @@
     pair = lax.all_gather(last, "tm_1")
     (send,) = call(chip_body, "chip", shape((chips, 8, units), F32))(pair, growth)
     arrived = everywhere(send, "tm_0")
-    (charge,) = call(charge_body, "charge", shape((hours, units), F32))(
-        arrived, pair, growth, chain, running
-    )
+    results = (gen, storage_next, dual, price)
+    charge, gen, storage_next, dual, price = pl.pallas_call(
+        charge_body,
+        name="charge",
+        out_specs=[hbm] * 5,
+        out_shape=[jax.ShapeDtypeStruct((hours, units), F32)]
+        + [jax.ShapeDtypeStruct(a.shape, F32) for a in results],
+        scratch_shapes=[pltpu.VMEM((hours, units), F32), pltpu.SemaphoreType.DMA((5,))],
+        compiler_params=pltpu.CompilerParams(vmem_limit_bytes=VMEM_LIMIT),
+    )(arrived, pair, growth, chain, running, *results)
     return (gen.T, storage_next.T, charge.T, dual.T, price[0])
 
 

time: 120 us -> 120 us (level)
  no operation moved by 1% of the time
where the time goes in v5:
time: 120 us
  blocking collectives  102 us (85%)
  Pallas kernels  16.8 us (14%)
    all_to_all x6, blocking collectives, everywhere(): return lax.all_to_all(blocks, axis, split_axis=0, concat_axis=0, tiled=True)  92.6 us
    all_gather x1, blocking collectives, per_device(): pair = lax.all_gather(last, 'tm_1')  9.61 us
    pallas_call x1, Pallas kernels, per_device(): pl.pallas_call(first_body, name='first', in_specs=[pl.BlockSpec(), hbm] +...  8.54 us
    pallas_call x1, Pallas kernels, per_device(): call(second_body, 'second', shape((net, hours, rows), BF16), shape((hours...  4.49 us

profile of v5, /device:TPU:1, one launch (start us, length us, event | category | flops | bytes accessed | tf_op | source)
XLA Modules:
  0.0 119.8 jit_solution(3064514925803661981)
XLA Ops:
  0.6 2.3 %pack.1 = (bf16[16,64,384]{2,1,0:T(8,128)(2,1)S(1)}, f32[1,1024]{1,0:T(1,128)S(1)}, f32[64,128]{1,0:T(8,128)S(1)}, f32[64,128]{1,0:T(8,128)S(1)}, f32[24,128]{1,...) custom-call(s32[1]{0:T(128)} %bitcast.chip, s32[1]{0:T(128)} %bitcast.1.core, ...), custom_call_target="tpu_custom_call" | custom-call | tf_op jit(solution)/shard_map/pack/pallas_call | solution.py:352
  2.9 19.6 %all_to_all.30.arrived = bf16[16,64,384]{2,1,0:T(8,128)(2,1)S(1)} all-to-all(bf16[16,64,384]{2,1,0:T(8,128)(2,1)S(1)} %get-tuple-element.41), channel_id=1, replica_groups=mesh['tm_0'=16,'tm_1'=2,'net'=16] {'net'}, dimensions={0} | all-to-all | bytes 1572864 | tf_op jit(solution)/shard_map/all_to_all | solution.py:305
  22.5 0.0 copy-start
  22.5 0.0 copy-start.1
  22.5 0.0 copy-start.2
  22.5 0.0 copy-start.3
  22.5 0.0 copy-start.4
  22.5 0.0 copy-start.5
  22.6 8.5 %first.1 = (bf16[16,64,256]{2,1,0:T(8,128)(2,1)S(1)}, f32[64,1024]{1,0:T(8,128)S(1)}, f32[64,1024]{1,0:T(8,128)S(1)}, f32[16,1024]{1,0:T(8,128)S(1)}, bf16[1024,4096]{1,0:T(8,128)(2,1)S(1)}) custom-call(bf16[16,64,384]{2,1,0:T(8,128)(2,1)S(1)} %all_to_all.30.arrived, bf16[1024,4096]{1,0:T(8,128)(2,1)} %ptdf.3, ...), custom_call_target="tpu_custom_call", output_to_operand_aliasing={{4}: (5, {})} | custom-call | tf_op jit(solution)/shard_map/first/pallas_call | solution.py:373
  31.1 0.0 copy-start.6
  31.1 12.0 %all_to_all.31.arrived = bf16[16,64,256]{2,1,0:T(8,128)(2,1)S(1)} all-to-all(bf16[16,64,256]{2,1,0:T(8,128)(2,1)S(1)} %get-tuple-element.46), channel_id=1, replica_groups=mesh['tm_0'=16,'tm_1'=2,'net'=16] {'net'}, dimensions={0} | all-to-all | bytes 1048576 | tf_op jit(solution)/shard_map/all_to_all | solution.py:305
  43.1 0.0 copy-done
  43.1 0.0 copy-done.1
  43.1 0.0 copy-done.2
  43.1 0.0 copy-done.3
  43.2 0.0 copy-done.4
  43.2 0.0 copy-done.5
  43.2 0.2 trial.1
  43.4 12.1 %all_to_all.32.arrived = bf16[16,72,256]{2,1,0:T(8,128)(2,1)S(1)} all-to-all(bf16[16,72,256]{2,1,0:T(8,128)(2,1)S(1)} %get-tuple-element.47), channel_id=1, replica_groups=mesh['tm_0'=16,'tm_1'=2,'net'=16] {'net'}, dimensions={0} | all-to-all | bytes 1179648 | tf_op jit(solution)/shard_map/all_to_all | solution.py:305
  55.5 4.5 %second.1 = (bf16[16,64,256]{2,1,0:T(8,128)(2,1)S(1)}, f32[64,1024]{1,0:T(8,128)S(1)}, f32[64,128]{1,0:T(8,128)S(1)}) custom-call(bf16[16,72,256]{2,1,0:T(8,128)(2,1)S(1)} %all_to_all.32.arrived, bf16[1024,4096]{1,0:T(8,128)(2,1)S(1)} %get-tuple-element.48.ptdf, f32[64,1024]{1,0:T(8,128)S(1)} %get-tuple-element.49.line_dual, ...), custom_call_target="tpu_custom_call" | custom-call | tf_op jit(solution)/shard_map/second/pallas_call | solution.py:398
  60.0 12.1 %all_to_all.33.arrived = bf16[16,64,256]{2,1,0:T(8,128)(2,1)S(1)} all-to-all(bf16[16,64,256]{2,1,0:T(8,128)(2,1)S(1)} %get-tuple-element.52), channel_id=1, replica_groups=mesh['tm_0'=16,'tm_1'=2,'net'=16] {'net'}, dimensions={0} | all-to-all | bytes 1048576 | tf_op jit(solution)/shard_map/all_to_all | solution.py:305
  72.1 0.3 last_trial.1
  72.4 9.2 %all_to_all.34.arrived = f32[16,8,128]{2,1,0:T(8,128)S(1)} all-to-all(f32[16,8,128]{2,1,0:T(8,128)S(1)} %get-tuple-element.55), channel_id=1, replica_groups=mesh['tm_0'=16,'tm_1'=2,'net'=16] {'net'}, dimensions={0} | all-to-all | bytes 131072 | tf_op jit(solution)/shard_map/all_to_all | solution.py:305
  81.6 0.0 copy-done.6
  81.6 0.2 finish.1
  81.8 9.6 %all-gather = f32[16,128]{1,0:T(8,128)S(1)} all-gather(f32[8,128]{1,0:T(8,128)S(1)} %get-tuple-element.59), channel_id=2, replica_groups=mesh['tm_0'=16,'tm_1'=2,'net'=16] {'tm_1'}, dimensions={0}, use_global_device_ids=true | all-gather | bytes 12288 | tf_op jit(solution)/shard_map/all_gather | solution.py:419
  91.4 27.6 %all_to_all.35.arrived = f32[16,8,128]{2,1,0:T(8,128)S(1)} all-to-all(f32[16,8,128]{2,1,0:T(8,128)S(1)} %chip.1), channel_id=1, replica_groups=mesh['tm_0'=16,'tm_1'=2,'net'=16] {'tm_0'}, dimensions={0} | all-to-all | bytes 131072 | tf_op jit(solution)/shard_map/all_to_all | solution.py:305
  119.0 0.8 charge.1
  (1 shorter events, 0.0 us)
Async XLA Ops:
  22.5 20.6 %copy-start = (f32[256,64]{0,1:T(8,128)S(1)}, f32[256,64]{0,1:T(8,128)}, u32[]{:S(2)}) copy-start(f32[256,64]{0,1:T(8,128)} %param.17) | copy-start | bytes 196612
  22.5 20.6 %copy-start.1 = (f32[128,64]{0,1:T(8,128)S(1)}, f32[128,64]{0,1:T(8,128)}, u32[]{:S(2)}) copy-start(f32[128,64]{0,1:T(8,128)} %param.21) | copy-start | bytes 98308
  22.5 20.6 %copy-start.2 = (f32[256,64]{0,1:T(8,128)S(1)}, f32[256,64]{0,1:T(8,128)}, u32[]{:S(2)}) copy-start(f32[256,64]{0,1:T(8,128)} %param.18) | copy-start | bytes 196612
  22.5 20.6 %copy-start.3 = (f32[256,64]{0,1:T(8,128)S(1)}, f32[256,64]{0,1:T(8,128)}, u32[]{:S(2)}) copy-start(f32[256,64]{0,1:T(8,128)} %param.19) | copy-start | bytes 196612
  22.5 20.6 %copy-start.4 = (f32[64]{0:T(128)S(1)}, f32[64]{0:T(128)}, u32[]{:S(2)}) copy-start(f32[64]{0:T(128)} %param.29) | copy-start | bytes 772
  22.5 20.6 %copy-start.5 = (f32[256]{0:T(256)S(1)}, f32[256]{0:T(256)}, u32[]{:S(2)}) copy-start(f32[256]{0:T(256)} %param.20) | copy-start | bytes 3076
  31.1 50.5 %copy-start.6 = (f32[128]{0:T(128)S(1)}, f32[128]{0:T(128)}, u32[]{:S(2)}) copy-start(f32[128]{0:T(128)} %param.22) | copy-start | bytes 1540

commit v6 on v5

--- a/solution.py
+++ b/solution.py
@@ -15,7 +15,6 @@
 
 F32 = jnp.float32
 VMEM_LIMIT = 16 << 20
-EARLY = 6
 BF16 = jnp.bfloat16
 NT = (((1,), (1,)), ((), ()))
 
@@ -58,8 +57,8 @@
 
 def pack_body(
     chip, core, gen_in, demand_in, storage_in, bus_in, dual_in, rating_in, index_in, leakage_in,
-    block_in, prices_in, initial_in, ptdf,
-    out, limit, growth, hour_price, chain, bus, line_dual, begun,
+    block_in, prices_in, initial_in,
+    out, limit, growth, hour_price, chain, bus, line_dual,
     gen, demand, storage, rating, index, leakage, hour_block, block_price, initial, sems
 ):
     pairs = (
@@ -78,9 +77,6 @@
     copies = [pltpu.make_async_copy(a, b, sems.at[k]) for k, (a, b) in enumerate(pairs)]
     for copy in copies:
         copy.start()
-    first_rows = pl.ds(0, begun.shape[0] * EARLY // 16)
-    early = pltpu.make_async_copy(ptdf.at[first_rows], begun.at[first_rows], sems.at[len(pairs)])
-    early.start()
     for copy in copies[:3]:
         copy.wait()
     rows = gen.shape[1]
@@ -95,7 +91,6 @@
     write_tables(
         here, rating, index, leakage, hour_block, block_price, initial, limit, growth, hour_price, chain
     )
-    early.wait()
 
 
 def write_tables(
@@ -138,12 +133,10 @@
 
 
 def first_body(
-    arrived, ptdf, bus, line_dual, limit, begun, parts, dual_out, unit_flow_out, row_sum, held,
+    arrived, ptdf, bus, line_dual, limit, parts, dual_out, unit_flow_out, row_sum, held,
     lefts, owned, hot, sem
 ):
-    early = held.shape[0] * EARLY // 16
-    rest = pl.ds(early, held.shape[0] - early)
-    copy = pltpu.make_async_copy(ptdf.at[rest], held.at[rest], sem)
+    copy = pltpu.make_async_copy(ptdf, held, sem)
     copy.start()
     count, hours, width = arrived.shape
     rows = parts.shape[2]
@@ -349,10 +342,10 @@
         initial,
     )
     smem, hbm = (pl.BlockSpec(memory_space=m) for m in (pltpu.SMEM, pltpu.HBM))
-    packed, limit, growth, hour_price, chain, bus, dual, begun = pl.pallas_call(
+    packed, limit, growth, hour_price, chain, bus, dual = pl.pallas_call(
         pack_body,
         name="pack",
-        in_specs=[smem, smem] + [hbm] * (len(sources) + 1),
+        in_specs=[smem, smem] + [hbm] * len(sources),
         out_shape=(
             jax.ShapeDtypeStruct((net, hours, rows + units), BF16),
             jax.ShapeDtypeStruct((1, lines), F32),
@@ -361,20 +354,18 @@
             jax.ShapeDtypeStruct((chips + 8, units), F32),
             jax.ShapeDtypeStruct((1, net * units), jnp.int32),
             jax.ShapeDtypeStruct((hours, lines), F32),
-            jax.ShapeDtypeStruct(ptdf.shape, BF16),
         ),
         scratch_shapes=[
             *(pltpu.VMEM(a.shape, a.dtype) for a in sources[:3] + sources[5:]),
-            pltpu.SemaphoreType.DMA((len(sources) + 1,)),
+            pltpu.SemaphoreType.DMA((len(sources),)),
         ],
         compiler_params=pltpu.CompilerParams(vmem_limit_bytes=VMEM_LIMIT),
-    )(chip, core, *(in_hbm(a) for a in (*sources, ptdf)))
+    )(chip, core, *(in_hbm(a) for a in sources))
     arrived = everywhere(packed, "net")
     parts, dual, unit_flow, row_sum, ptdf = pl.pallas_call(
         first_body,
         name="first",
-        in_specs=[pl.BlockSpec(), hbm] + [pl.BlockSpec()] * 4,
-        input_output_aliases={5: 4},
+        in_specs=[pl.BlockSpec(), hbm] + [pl.BlockSpec()] * 3,
         out_shape=(
             jax.ShapeDtypeStruct((net, hours, rows), BF16),
             jax.ShapeDtypeStruct((hours, lines), F32),
@@ -389,7 +380,7 @@
             pltpu.SemaphoreType.DMA(()),
         ],
         compiler_params=pltpu.CompilerParams(vmem_limit_bytes=VMEM_LIMIT),
-    )(arrived, in_hbm(ptdf), bus, dual, limit, begun)
+    )(arrived, in_hbm(ptdf), bus, dual, limit)
     arrived = everywhere(parts, "net")
     send, trial = call(
         trial_body, "trial", shape((net, hours + 8, rows), BF16), shape((hours, rows), F32)

time: 120 us -> 119 us (level)
  no operation moved by 1% of the time
where the time goes in v6:
time: 119 us
  blocking collectives  102 us (86%)
  Pallas kernels  15.9 us (13%)
    all_to_all x6, blocking collectives, everywhere(): return lax.all_to_all(blocks, axis, split_axis=0, concat_axis=0, tiled=True)  92.6 us
    all_gather x1, blocking collectives, per_device(): pair = lax.all_gather(last, 'tm_1')  9.62 us
    pallas_call x1, Pallas kernels, per_device(): pl.pallas_call(first_body, name='first', in_specs=[pl.BlockSpec(), hbm] +...  8.25 us
    pallas_call x1, Pallas kernels, per_device(): call(second_body, 'second', shape((net, hours, rows), BF16), shape((hours...  4.49 us

profile of v6, /device:TPU:1, one launch (start us, length us, event | category | flops | bytes accessed | tf_op | source)
XLA Modules:
  0.0 118.9 jit_solution(18319097742679704930)
XLA Ops:
  0.6 0.0 copy-start.2
  0.6 0.0 copy-start.1
  0.7 0.0 copy-start
  0.7 0.0 copy-start.4
  0.7 0.0 copy-start.5
  0.7 0.0 copy-start.3
  0.7 1.7 %pack.1 = (bf16[16,64,384]{2,1,0:T(8,128)(2,1)S(1)}, f32[1,1024]{1,0:T(1,128)S(1)}, f32[64,128]{1,0:T(8,128)S(1)}, f32[64,128]{1,0:T(8,128)S(1)}, f32[24,128]{1,...) custom-call(s32[1]{0:T(128)} %bitcast.chip, s32[1]{0:T(128)} %bitcast.1.core, f32[64,256]{1,0:T(8,128)} %bitcast.30, ...), custom_call_target="tpu_custom_call" | custom-call | tf_op jit(solution)/shard_map/pack/pallas_call | solution.py:345
  2.4 19.6 %all_to_all.30.arrived = bf16[16,64,384]{2,1,0:T(8,128)(2,1)S(1)} all-to-all(bf16[16,64,384]{2,1,0:T(8,128)(2,1)S(1)} %get-tuple-element.40), channel_id=1, replica_groups=mesh['tm_0'=16,'tm_1'=2,'net'=16] {'net'}, dimensions={0} | all-to-all | bytes 1572864 | tf_op jit(solution)/shard_map/all_to_all | solution.py:298
  22.0 8.2 %first.1 = (bf16[16,64,256]{2,1,0:T(8,128)(2,1)S(1)}, f32[64,1024]{1,0:T(8,128)S(1)}, f32[64,1024]{1,0:T(8,128)S(1)}, f32[16,1024]{1,0:T(8,128)S(1)}, bf16[1024,4096]{1,0:T(8,128)(2,1)S(1)}) custom-call(bf16[16,64,384]{2,1,0:T(8,128)(2,1)S(1)} %all_to_all.30.arrived, bf16[1024,4096]{1,0:T(8,128)(2,1)} %ptdf.1, s32[1,2048]{1,0:T(1,128)S(1)} %get-tuple-element.41.bus, ...), custom_call_target="tpu_custom_call" | custom-call | tf_op jit(solution)/shard_map/first/pallas_call | solution.py:365
  30.2 0.0 copy-start.6
  30.2 12.0 %all_to_all.31.arrived = bf16[16,64,256]{2,1,0:T(8,128)(2,1)S(1)} all-to-all(bf16[16,64,256]{2,1,0:T(8,128)(2,1)S(1)} %get-tuple-element.44), channel_id=1, replica_groups=mesh['tm_0'=16,'tm_1'=2,'net'=16] {'net'}, dimensions={0} | all-to-all | bytes 1048576 | tf_op jit(solution)/shard_map/all_to_all | solution.py:298
  42.3 0.0 copy-done.2
  42.3 0.0 copy-done.1
  42.3 0.0 copy-done
  42.3 0.0 copy-done.4
  42.3 0.0 copy-done.5
  42.3 0.0 copy-done.3
  42.3 0.2 trial.1
  42.5 12.1 %all_to_all.32.arrived = bf16[16,72,256]{2,1,0:T(8,128)(2,1)S(1)} all-to-all(bf16[16,72,256]{2,1,0:T(8,128)(2,1)S(1)} %get-tuple-element.45), channel_id=1, replica_groups=mesh['tm_0'=16,'tm_1'=2,'net'=16] {'net'}, dimensions={0} | all-to-all | bytes 1179648 | tf_op jit(solution)/shard_map/all_to_all | solution.py:298
  54.6 4.5 %second.1 = (bf16[16,64,256]{2,1,0:T(8,128)(2,1)S(1)}, f32[64,1024]{1,0:T(8,128)S(1)}, f32[64,128]{1,0:T(8,128)S(1)}) custom-call(bf16[16,72,256]{2,1,0:T(8,128)(2,1)S(1)} %all_to_all.32.arrived, bf16[1024,4096]{1,0:T(8,128)(2,1)S(1)} %get-tuple-element.46.ptdf, f32[64,1024]{1,0:T(8,128)S(1)} %get-tuple-element.47.line_dual, ...), custom_call_target="tpu_custom_call" | custom-call | tf_op jit(solution)/shard_map/second/pallas_call | solution.py:389
  59.1 12.1 %all_to_all.33.arrived = bf16[16,64,256]{2,1,0:T(8,128)(2,1)S(1)} all-to-all(bf16[16,64,256]{2,1,0:T(8,128)(2,1)S(1)} %get-tuple-element.50), channel_id=1, replica_groups=mesh['tm_0'=16,'tm_1'=2,'net'=16] {'net'}, dimensions={0} | all-to-all | bytes 1048576 | tf_op jit(solution)/shard_map/all_to_all | solution.py:298
  71.2 0.3 last_trial.1
  71.5 9.2 %all_to_all.34.arrived = f32[16,8,128]{2,1,0:T(8,128)S(1)} all-to-all(f32[16,8,128]{2,1,0:T(8,128)S(1)} %get-tuple-element.53), channel_id=1, replica_groups=mesh['tm_0'=16,'tm_1'=2,'net'=16] {'net'}, dimensions={0} | all-to-all | bytes 131072 | tf_op jit(solution)/shard_map/all_to_all | solution.py:298
  80.7 0.0 copy-done.6
  80.7 0.2 finish.1
  80.9 9.6 %all-gather = f32[16,128]{1,0:T(8,128)S(1)} all-gather(f32[8,128]{1,0:T(8,128)S(1)} %get-tuple-element.57), channel_id=2, replica_groups=mesh['tm_0'=16,'tm_1'=2,'net'=16] {'tm_1'}, dimensions={0}, use_global_device_ids=true | all-gather | bytes 12288 | tf_op jit(solution)/shard_map/all_gather | solution.py:410
  90.5 27.6 %all_to_all.35.arrived = f32[16,8,128]{2,1,0:T(8,128)S(1)} all-to-all(f32[16,8,128]{2,1,0:T(8,128)S(1)} %chip.1), channel_id=1, replica_groups=mesh['tm_0'=16,'tm_1'=2,'net'=16] {'tm_0'}, dimensions={0} | all-to-all | bytes 131072 | tf_op jit(solution)/shard_map/all_to_all | solution.py:298
  118.1 0.8 charge.1
  (1 shorter events, 0.0 us)
Async XLA Ops:
  0.6 41.6 %copy-start.2 = (f32[256,64]{0,1:T(8,128)S(1)}, f32[256,64]{0,1:T(8,128)}, u32[]{:S(2)}) copy-start(f32[256,64]{0,1:T(8,128)} %param.18) | copy-start | bytes 196612
  0.6 41.6 %copy-start.1 = (f32[128,64]{0,1:T(8,128)S(1)}, f32[128,64]{0,1:T(8,128)}, u32[]{:S(2)}) copy-start(f32[128,64]{0,1:T(8,128)} %param.21) | copy-start | bytes 98308
  0.7 41.6 %copy-start = (f32[256,64]{0,1:T(8,128)S(1)}, f32[256,64]{0,1:T(8,128)}, u32[]{:S(2)}) copy-start(f32[256,64]{0,1:T(8,128)} %param.17) | copy-start | bytes 196612
  0.7 41.6 %copy-start.4 = (f32[64]{0:T(128)S(1)}, f32[64]{0:T(128)}, u32[]{:S(2)}) copy-start(f32[64]{0:T(128)} %param.29) | copy-start | bytes 772
  0.7 41.6 %copy-start.5 = (f32[256]{0:T(256)S(1)}, f32[256]{0:T(256)}, u32[]{:S(2)}) copy-start(f32[256]{0:T(256)} %param.20) | copy-start | bytes 3076
  0.7 41.6 %copy-start.3 = (f32[256,64]{0,1:T(8,128)S(1)}, f32[256,64]{0,1:T(8,128)}, u32[]{:S(2)}) copy-start(f32[256,64]{0,1:T(8,128)} %param.19) | copy-start | bytes 196612
  30.2 50.4 %copy-start.6 = (f32[128]{0:T(128)S(1)}, f32[128]{0:T(128)}, u32[]{:S(2)}) copy-start(f32[128]{0:T(128)} %param.22) | copy-start | bytes 1540

commit v7 on v6

--- a/solution.py
+++ b/solution.py
@@ -56,24 +56,9 @@
 
 
 def pack_body(
-    chip, core, gen_in, demand_in, storage_in, bus_in, dual_in, rating_in, index_in, leakage_in,
-    block_in, prices_in, initial_in,
-    out, limit, growth, hour_price, chain, bus, line_dual,
-    gen, demand, storage, rating, index, leakage, hour_block, block_price, initial, sems
-):
-    pairs = (
-        (gen_in, gen),
-        (demand_in, demand),
-        (storage_in, storage),
-        (rating_in, rating),
-        (index_in, index),
-        (leakage_in, leakage),
-        (block_in, hour_block),
-        (prices_in, block_price),
-        (initial_in, initial),
-        (bus_in, bus),
-        (dual_in, line_dual),
-    )
+    gen_in, demand_in, storage_in, bus_in, out, bus, gen, demand, storage, sems
+):
+    pairs = ((gen_in, gen), (demand_in, demand), (storage_in, storage), (bus_in, bus))
     copies = [pltpu.make_async_copy(a, b, sems.at[k]) for k, (a, b) in enumerate(pairs)]
     for copy in copies:
         copy.start()
@@ -87,10 +72,6 @@
         out[d, :, rows:] = units
     for copy in copies[3:]:
         copy.wait()
-    here = chip[0], core[0]
-    write_tables(
-        here, rating, index, leakage, hour_block, block_price, initial, limit, growth, hour_price, chain
-    )
 
 
 def write_tables(
@@ -133,9 +114,22 @@
 
 
 def first_body(
-    arrived, ptdf, bus, line_dual, limit, parts, dual_out, unit_flow_out, row_sum, held,
-    lefts, owned, hot, sem
-):
+    chip, core, arrived, bus, ptdf, dual_in, rating_in, index_in, leakage_in, block_in, prices_in, initial_in,
+    parts, dual_out, unit_flow_out, row_sum, limit, growth, hour_price, chain, held,
+    line_dual, rating, index, leakage, hour_block, block_price, initial, lefts, owned, hot, sem, sems
+):
+    pairs = (
+        (rating_in, rating),
+        (index_in, index),
+        (leakage_in, leakage),
+        (block_in, hour_block),
+        (prices_in, block_price),
+        (initial_in, initial),
+        (dual_in, line_dual),
+    )
+    small = [pltpu.make_async_copy(a, b, sems.at[k]) for k, (a, b) in enumerate(pairs)]
+    for each in small:
+        each.start()
     copy = pltpu.make_async_copy(ptdf, held, sem)
     copy.start()
     count, hours, width = arrived.shape
@@ -161,6 +155,12 @@
         at = slice(d * rows, (d + 1) * rows)
         lefts[hours : 2 * hours, at] = high
         lefts[2 * hours : 3 * hours, at] = (part - high.astype(F32)).astype(BF16)
+    for each in small:
+        each.wait()
+    here = chip[0], core[0]
+    write_tables(
+        here, rating, index, leakage, hour_block, block_price, initial, limit, growth, hour_price, chain
+    )
     copy.wait()
     products = lax.dot_general(lefts[...], held[...], NT, preferred_element_type=F32)
     unit_flow = products[hours : 2 * hours] + products[2 * hours : 3 * hours]
@@ -328,12 +328,24 @@
     chip, core, gen = lax.optimization_barrier(
         (lax.axis_index("tm_0").reshape(1), lax.axis_index("tm_1").reshape(1), gen)
     )
+    sources = (gen, demand, held, storage_bus[None])
+    smem, hbm = (pl.BlockSpec(memory_space=m) for m in (pltpu.SMEM, pltpu.HBM))
+    packed, bus = pl.pallas_call(
+        pack_body,
+        name="pack",
+        in_specs=[hbm] * len(sources),
+        out_shape=(
+            jax.ShapeDtypeStruct((net, hours, rows + units), BF16),
+            jax.ShapeDtypeStruct((1, net * units), jnp.int32),
+        ),
+        scratch_shapes=[
+            *(pltpu.VMEM(a.shape, a.dtype) for a in sources[:3]),
+            pltpu.SemaphoreType.DMA((len(sources),)),
+        ],
+        compiler_params=pltpu.CompilerParams(vmem_limit_bytes=VMEM_LIMIT),
+    )(*(in_hbm(a) for a in sources))
+    arrived = everywhere(packed, "net")
     sources = (
-        gen,
-        demand,
-        held,
-        storage_bus[None],
-        dual,
         rating.reshape(-1, 128),
         line_index[None],
         leakage[None],
@@ -341,46 +353,31 @@
         block_price[None],
         initial,
     )
-    smem, hbm = (pl.BlockSpec(memory_space=m) for m in (pltpu.SMEM, pltpu.HBM))
-    packed, limit, growth, hour_price, chain, bus, dual = pl.pallas_call(
-        pack_body,
-        name="pack",
-        in_specs=[smem, smem] + [hbm] * len(sources),
-        out_shape=(
-            jax.ShapeDtypeStruct((net, hours, rows + units), BF16),
-            jax.ShapeDtypeStruct((1, lines), F32),
-            jax.ShapeDtypeStruct((hours, units), F32),
-            jax.ShapeDtypeStruct((hours, units), F32),
-            jax.ShapeDtypeStruct((chips + 8, units), F32),
-            jax.ShapeDtypeStruct((1, net * units), jnp.int32),
-            jax.ShapeDtypeStruct((hours, lines), F32),
-        ),
-        scratch_shapes=[
-            *(pltpu.VMEM(a.shape, a.dtype) for a in sources[:3] + sources[5:]),
-            pltpu.SemaphoreType.DMA((len(sources),)),
-        ],
-        compiler_params=pltpu.CompilerParams(vmem_limit_bytes=VMEM_LIMIT),
-    )(chip, core, *(in_hbm(a) for a in sources))
-    arrived = everywhere(packed, "net")
-    parts, dual, unit_flow, row_sum, ptdf = pl.pallas_call(
+    parts, dual, unit_flow, row_sum, limit, growth, hour_price, chain, ptdf = pl.pallas_call(
         first_body,
         name="first",
-        in_specs=[pl.BlockSpec(), hbm] + [pl.BlockSpec()] * 3,
+        in_specs=[smem, smem, pl.BlockSpec(), pl.BlockSpec()] + [hbm] * 8,
         out_shape=(
             jax.ShapeDtypeStruct((net, hours, rows), BF16),
             jax.ShapeDtypeStruct((hours, lines), F32),
             jax.ShapeDtypeStruct((hours, lines), F32),
             jax.ShapeDtypeStruct((net, lines), F32),
+            jax.ShapeDtypeStruct((1, lines), F32),
+            jax.ShapeDtypeStruct((hours, units), F32),
+            jax.ShapeDtypeStruct((hours, units), F32),
+            jax.ShapeDtypeStruct((chips + 8, units), F32),
             jax.ShapeDtypeStruct(ptdf.shape, BF16),
         ),
         scratch_shapes=[
+            *(pltpu.VMEM(a.shape, a.dtype) for a in (dual, *sources)),
             pltpu.VMEM((3 * hours + net, net * rows), BF16),
             pltpu.VMEM((net * hours, net * units), BF16),
             pltpu.VMEM((rows, net * units), BF16),
             pltpu.SemaphoreType.DMA(()),
+            pltpu.SemaphoreType.DMA((7,)),
         ],
         compiler_params=pltpu.CompilerParams(vmem_limit_bytes=VMEM_LIMIT),
-    )(arrived, in_hbm(ptdf), bus, dual, limit)
+    )(chip, core, arrived, bus, *(in_hbm(a) for a in (ptdf, dual, *sources)))
     arrived = everywhere(parts, "net")
     send, trial = call(
         trial_body, "trial", shape((net, hours + 8, rows), BF16), shape((hours, rows), F32)

time: 119 us -> 120 us (level)
  no operation moved by 1% of the time
where the time goes in v7:
time: 120 us; the launch traced here: 119 us
  blocking collectives  102 us (85%)
  Pallas kernels  16.5 us (14%)
    all_to_all x6, blocking collectives, everywhere(): return lax.all_to_all(blocks, axis, split_axis=0, concat_axis=0, tiled=True)  92.6 us
    all_gather x1, blocking collectives, per_device(): pair = lax.all_gather(last, 'tm_1')  9.61 us
    pallas_call x1, Pallas kernels, per_device(): pl.pallas_call(first_body, name='first', in_specs=[smem, smem, pl.BlockSp...  9.42 us
    pallas_call x1, Pallas kernels, per_device(): call(second_body, 'second', shape((net, hours, rows), BF16), shape((hours...  4.49 us

profile of v7, /device:TPU:1, one launch (start us, length us, event | category | flops | bytes accessed | tf_op | source)
XLA Modules:
  0.0 119.5 jit_solution(4384947175801027236)
XLA Ops:
  0.6 0.0 copy-start.2
  0.6 0.0 copy-start.1
  0.7 0.0 copy-start
  0.7 0.0 copy-start.4
  0.7 0.0 copy-start.5
  0.7 0.0 copy-start.3
  0.7 1.1 pack.1
  1.8 19.6 %all_to_all.30.arrived = bf16[16,64,384]{2,1,0:T(8,128)(2,1)S(1)} all-to-all(bf16[16,64,384]{2,1,0:T(8,128)(2,1)S(1)} %get-tuple-element.39), channel_id=1, replica_groups=mesh['tm_0'=16,'tm_1'=2,'net'=16] {'net'}, dimensions={0} | all-to-all | bytes 1572864 | tf_op jit(solution)/shard_map/all_to_all | solution.py:298
  21.4 9.4 %first.1 = (bf16[16,64,256]{2,1,0:T(8,128)(2,1)S(1)}, f32[64,1024]{1,0:T(8,128)S(1)}, f32[64,1024]{1,0:T(8,128)S(1)}, f32[16,1024]{1,0:T(8,128)S(1)}, f32[1,1024...) custom-call(s32[1]{0:T(128)} %bitcast.chip, ...), custom_call_target="tpu_custom_call" | custom-call | tf_op jit(solution)/shard_map/first/pallas_call | solution.py:356
  30.8 0.0 copy-start.6
  30.8 12.0 %all_to_all.31.arrived = bf16[16,64,256]{2,1,0:T(8,128)(2,1)S(1)} all-to-all(bf16[16,64,256]{2,1,0:T(8,128)(2,1)S(1)} %get-tuple-element.41), channel_id=1, replica_groups=mesh['tm_0'=16,'tm_1'=2,'net'=16] {'net'}, dimensions={0} | all-to-all | bytes 1048576 | tf_op jit(solution)/shard_map/all_to_all | solution.py:298
  42.9 0.0 copy-done.2
  42.9 0.0 copy-done.1
  42.9 0.0 copy-done
  42.9 0.0 copy-done.4
  42.9 0.0 copy-done.5
  42.9 0.0 copy-done.3
  42.9 0.2 trial.1
  43.1 12.1 %all_to_all.32.arrived = bf16[16,72,256]{2,1,0:T(8,128)(2,1)S(1)} all-to-all(bf16[16,72,256]{2,1,0:T(8,128)(2,1)S(1)} %get-tuple-element.42), channel_id=1, replica_groups=mesh['tm_0'=16,'tm_1'=2,'net'=16] {'net'}, dimensions={0} | all-to-all | bytes 1179648 | tf_op jit(solution)/shard_map/all_to_all | solution.py:298
  55.2 4.5 %second.1 = (bf16[16,64,256]{2,1,0:T(8,128)(2,1)S(1)}, f32[64,1024]{1,0:T(8,128)S(1)}, f32[64,128]{1,0:T(8,128)S(1)}) custom-call(bf16[16,72,256]{2,1,0:T(8,128)(2,1)S(1)} %all_to_all.32.arrived, bf16[1024,4096]{1,0:T(8,128)(2,1)S(1)} %get-tuple-element.43.ptdf, f32[64,1024]{1,0:T(8,128)S(1)} %get-tuple-element.44.line_dual, ...), custom_call_target="tpu_custom_call" | custom-call | tf_op jit(solution)/shard_map/second/pallas_call | solution.py:386
  59.7 12.1 %all_to_all.33.arrived = bf16[16,64,256]{2,1,0:T(8,128)(2,1)S(1)} all-to-all(bf16[16,64,256]{2,1,0:T(8,128)(2,1)S(1)} %get-tuple-element.48), channel_id=1, replica_groups=mesh['tm_0'=16,'tm_1'=2,'net'=16] {'net'}, dimensions={0} | all-to-all | bytes 1048576 | tf_op jit(solution)/shard_map/all_to_all | solution.py:298
  71.8 0.3 last_trial.1
  72.1 9.2 %all_to_all.34.arrived = f32[16,8,128]{2,1,0:T(8,128)S(1)} all-to-all(f32[16,8,128]{2,1,0:T(8,128)S(1)} %get-tuple-element.51), channel_id=1, replica_groups=mesh['tm_0'=16,'tm_1'=2,'net'=16] {'net'}, dimensions={0} | all-to-all | bytes 131072 | tf_op jit(solution)/shard_map/all_to_all | solution.py:298
  81.3 0.0 copy-done.6
  81.3 0.2 finish.1
  81.5 9.6 %all-gather = f32[16,128]{1,0:T(8,128)S(1)} all-gather(f32[8,128]{1,0:T(8,128)S(1)} %get-tuple-element.55), channel_id=2, replica_groups=mesh['tm_0'=16,'tm_1'=2,'net'=16] {'tm_1'}, dimensions={0}, use_global_device_ids=true | all-gather | bytes 12288 | tf_op jit(solution)/shard_map/all_gather | solution.py:407
  91.2 27.6 %all_to_all.35.arrived = f32[16,8,128]{2,1,0:T(8,128)S(1)} all-to-all(f32[16,8,128]{2,1,0:T(8,128)S(1)} %chip.1), channel_id=1, replica_groups=mesh['tm_0'=16,'tm_1'=2,'net'=16] {'tm_0'}, dimensions={0} | all-to-all | bytes 131072 | tf_op jit(solution)/shard_map/all_to_all | solution.py:298
  118.7 0.8 charge.1
  (1 shorter events, 0.0 us)
Async XLA Ops:
  0.6 42.2 %copy-start.2 = (f32[256,64]{0,1:T(8,128)S(1)}, f32[256,64]{0,1:T(8,128)}, u32[]{:S(2)}) copy-start(f32[256,64]{0,1:T(8,128)} %param.18) | copy-start | bytes 196612
  0.6 42.2 %copy-start.1 = (f32[128,64]{0,1:T(8,128)S(1)}, f32[128,64]{0,1:T(8,128)}, u32[]{:S(2)}) copy-start(f32[128,64]{0,1:T(8,128)} %param.21) | copy-start | bytes 98308
  0.7 42.2 %copy-start = (f32[256,64]{0,1:T(8,128)S(1)}, f32[256,64]{0,1:T(8,128)}, u32[]{:S(2)}) copy-start(f32[256,64]{0,1:T(8,128)} %param.17) | copy-start | bytes 196612
  0.7 42.2 %copy-start.4 = (f32[64]{0:T(128)S(1)}, f32[64]{0:T(128)}, u32[]{:S(2)}) copy-start(f32[64]{0:T(128)} %param.29) | copy-start | bytes 772
  0.7 42.2 %copy-start.5 = (f32[256]{0:T(256)S(1)}, f32[256]{0:T(256)}, u32[]{:S(2)}) copy-start(f32[256]{0:T(256)} %param.20) | copy-start | bytes 3076
  0.7 42.2 %copy-start.3 = (f32[256,64]{0,1:T(8,128)S(1)}, f32[256,64]{0,1:T(8,128)}, u32[]{:S(2)}) copy-start(f32[256,64]{0,1:T(8,128)} %param.19) | copy-start | bytes 196612
  30.8 50.5 %copy-start.6 = (f32[128]{0:T(128)S(1)}, f32[128]{0:T(128)}, u32[]{:S(2)}) copy-start(f32[128]{0:T(128)} %param.22) | copy-start | bytes 1540
